TPU v7x, 512 devices: a whole 4x4x16 slice. The times are simulated.
512 devices in a mesh: pos: 16 (over z_lo, x), slab: 32 (over z_hi, y, core).
Axes of the slice: x: 4, y: 4, z: 16 (z_hi: 4, z_lo: 4; z = z_hi * 4 + z_lo), core: 2. Of those that a mesh axis runs over, the one named last changes fastest.
Arguments:
- labels: int32 [64, 256, 256], P('slab'), may hold values from 0 to 3
- magnet_mask: int32 [64, 256, 256], P('slab'), may hold values 0 or 1
- reluctivity: float32 [4], replicated, may hold values from 0.3 to 3
- rotor_shift: int32 [16], P('pos'), may hold values from 0 to 255
- potential: float32 [16, 64, 256, 256], P('pos', 'slab'), may hold values from -6 to 6
- adjoint_load: float32 [16, 64, 256, 256], P('pos', 'slab'), may hold values from -40 to 40
Outputs:
- shape_gradient: float32 [64, 256, 256], P('slab')
- adjoint: float32 [16, 64, 256, 256], P('pos', 'slab')
All inputs are finite; a program needn't handle non-finite values. No bound on the sum of `magnet_mask` on one device may be relied on, other than what follows from the above.
Results may differ from a plain program's by a relative error of at most 0.0003.
Values sent between devices are 32-bit elements; how exact they have to be, the bound alone decides.
A program may use at most 64 MiB of HBM per device.

v0:
```python
import jax
import jax.numpy as jnp
from jax import lax
from jax.sharding import PartitionSpec as P

ITERS = 2


diagonal_shift = 0.5


def padded(shard, sides, width):
    for axis, dim in sides:
        size, length = (lax.axis_size(axis), shard.shape[dim])
        up = [(i, (i + 1) % size) for i in range(size - 1)]
        down = [(j, i) for i, j in up]
        last = lax.slice_in_dim(shard, length - width, length, axis=dim)
        first = lax.slice_in_dim(shard, 0, width, axis=dim)
        before = lax.ppermute(last, axis, up)
        after = lax.ppermute(first, axis, down)
        shard = jnp.concatenate([before, shard, after], axis=dim)
    return shard


def material_field(labels, reluctivity, offset):
    rotated = jnp.roll(labels, offset, axis=2)
    radial = lax.broadcasted_iota(jnp.int32, labels.shape, 1)
    material = jnp.where(radial < labels.shape[1] // 2, rotated, labels)
    result = jnp.zeros(labels.shape, jnp.float32)
    for index in range(4):
        result = result + (material == index).astype(jnp.float32) * reluctivity[index]
    return result


def apply_operator(field, padded_field, relief, padded_relief):
    result = diagonal_shift * field
    result = result + 0.5 * (relief + padded_relief[2:]) * (field - padded_field[2:])
    result = result + 0.5 * (relief + padded_relief[:-2]) * (field - padded_field[:-2])
    radial_field = jnp.pad(field, ((0, 0), (1, 1), (0, 0)))
    radial_relief = jnp.pad(relief, ((0, 0), (1, 1), (0, 0)))
    result = result + 0.5 * (relief + radial_relief[:, 2:]) * (field - radial_field[:, 2:])
    result = result + 0.5 * (relief + radial_relief[:, :-2]) * (field - radial_field[:, :-2])
    for offset in (1, -1):
        result = result + 0.5 * (relief + jnp.roll(relief, offset, 2)) * (
            field - jnp.roll(field, offset, 2)
        )
    return result


def gradient_term(stacked, padded_stack, relief, magnet_mask):
    axial = 0.5 * (padded_stack[:, 2:] - padded_stack[:, :-2])
    radial_pad = jnp.pad(stacked, ((0, 0), (0, 0), (1, 1), (0, 0)))
    radial = 0.5 * (radial_pad[:, :, 2:] - radial_pad[:, :, :-2])
    angular = 0.5 * (jnp.roll(stacked, -1, 3) - jnp.roll(stacked, 1, 3))
    inner = axial[0] * axial[1] + radial[0] * radial[1] + angular[0] * angular[1]
    square = axial[0] * axial[0] + radial[0] * radial[0] + angular[0] * angular[0]
    return magnet_mask.astype(jnp.float32) * relief * (inner + 0.5 * square)


def squares(residual):
    return lax.psum(jnp.sum(residual * residual), "slab")


def local(labels, magnet_mask, reluctivity, rotor_shift, potential, adjoint_load):
    relief = material_field(labels, reluctivity, rotor_shift[0])
    padded_relief = padded(relief, (("slab", 0),), 1)
    solution = jnp.zeros(relief.shape, jnp.float32)
    residual = adjoint_load[0]
    direction = residual
    norm_now = squares(residual)
    for iteration in range(ITERS):
        padded_field = padded(direction, (("slab", 0),), 1)
        image = apply_operator(direction, padded_field, relief, padded_relief)
        alpha = norm_now / lax.psum(jnp.sum(direction * image), "slab")
        solution = solution + alpha * direction
        residual = residual - alpha * image
        norm_next = squares(residual)
        direction = residual + norm_next / norm_now * direction
        norm_now = norm_next
    stacked = jnp.stack([potential[0], solution])
    padded_stack = padded(stacked, (("slab", 1),), 1)
    contribution = gradient_term(stacked, padded_stack, relief, magnet_mask)
    summed = lax.psum(contribution, "pos")
    return (summed / lax.axis_size("pos"), solution[None])


def solution(mesh):
    return jax.shard_map(
        local,
        mesh=mesh,
        in_specs=(
            P("slab", None, None),
            P("slab", None, None),
            P(),
            P("pos"),
            P("pos", "slab", None, None),
            P("pos", "slab", None, None),
        ),
        out_specs=(P("slab", None, None), P("pos", "slab", None, None)),
        check_vma=False,
    )
```

profile of v0, /device:TPU:8, one launch (start us, length us, event | category | flops | bytes accessed | tf_op | source)
XLA Modules:
  0.0 558.3 jit_solution(6151440687633539958)
XLA Ops:
  7.2 1.1 slice_bitcast_fusion.1
  8.3 1.9 collective-permute-start.3
  11.7 3.0 select_add_fusion
  14.7 3.6 collective-permute-start.2
  18.3 2.0 collective-permute-start.1
  20.3 5.6 %collective-permute-start = (f32[1,256,256]{2,1,0:T(8,128)S(1)}, f32[1,256,256]{2,1,0:T(8,128)S(1)}, u32[]{:S(2)}, u32[]{:S(2)}) collective-permute-start(f32[1,256,256]{2,1,0:T(8,128)S(1)} %get-tuple-element.21), channel_id=1, source_target_pairs={{1,0},{2,1},{3,2},{4,3},{5,4},{6,5},{7,6},{8,7},{9,8},{10,9},{11,1... | collective-permute-start | bytes 786440 | tf_op jit(solution)/shard_map/ppermute | solution.py:20
  26.5 3.3 collective-permute-done
  29.7 2.6 multiply_reduce_fusion.1
  32.3 91.9 %all-reduce.4 = (f32[]{:T(128)}, f32[]{:T(128)}) all-reduce(f32[]{:T(128)} %get-tuple-element.3, f32[]{:T(128)} %get-tuple-element.2), channel_id=1, replica_groups=mesh['pos'=16,'slab'=32] {'slab'}, use_global_device_ids=true, to_apply=%region_1.2 | all-reduce | flops 2 | bytes 16 | tf_op jit(solution)/shard_map/psum | solution.py:61
  125.6 0.7 multiply_reduce_fusion
  126.3 90.4 %psum.37 = f32[]{:T(128)} all-reduce(f32[]{:T(128)} %multiply_reduce_fusion), channel_id=1, replica_groups=mesh['pos'=16,'slab'=32] {'slab'}, use_global_device_ids=true, to_apply=%region_5.6 | all-reduce | flops 1 | bytes 8 | tf_op jit(solution)/shard_map/psum | solution.py:61
  218.3 2.5 collective-permute-start.5
  220.8 3.2 collective-permute-start.4
  224.2 1.8 collective-permute-done.5
  226.0 5.7 %collective-permute-done.4 = f32[1,256,256]{2,1,0:T(8,128)S(1)} collective-permute-done((f32[1,256,256]{2,1,0:T(8,128)S(1)}, f32[1,256,256]{2,1,0:T(8,128)S(1)}, u32[]{:S(2)}, u32[]{:S(2)}) %collective-permute-start.4) | collective-permute-done | bytes 262176 | tf_op jit(solution)/shard_map/ppermute | solution.py:20
  231.7 1.5 fusion.47
  233.2 89.6 %psum.38 = f32[]{:T(128)} all-reduce(f32[]{:T(128)} %fusion.47), channel_id=1, replica_groups=mesh['pos'=16,'slab'=32] {'slab'}, use_global_device_ids=true, to_apply=%region_7.8 | all-reduce | flops 1 | bytes 8 | tf_op jit(solution)/shard_map/psum | solution.py:74
  324.3 8.0 %collective-permute-start.7 = (f32[2,1,256,256]{3,2,1,0:T(8,128)S(1)}, f32[2,1,256,256]{3,2,1,0:T(8,128)S(1)}, u32[]{:S(2)}, u32[]{:S(2)}) collective-permute-start(f32[2,1,256,256]{3,2,1,0:T(8,128)S(1)} %get-tuple-element.10), channel_id=1, source_target_pairs={{0,1},{1,2},{2,3},{3,4},{4,5},{5,6},{6,7},{7,8},{8,9},{9,10},{10,1... | collective-permute-start | bytes 1572872 | tf_op jit(solution)/shard_map/ppermute | solution.py:19
  332.3 1.9 collective-permute-start.6
  335.3 5.6 %collective-permute-done.6 = f32[2,1,256,256]{3,2,1,0:T(8,128)S(1)} collective-permute-done((f32[2,1,256,256]{3,2,1,0:T(8,128)S(1)}, f32[2,1,256,256]{3,2,1,0:T(8,128)S(1)}, u32[]{:S(2)}, u32[]{:S(2)}) %collective-permute-start.6) | collective-permute-done | bytes 524320 | tf_op jit(solution)/shard_map/ppermute | solution.py:20
  341.4 0.8 copy-done.4
  342.4 4.0 fusion.14
  346.4 203.2 %all-reduce.7.cloned.1.call-done = f32[2,256,256]{2,1,0:T(8,128)} async-done(((f32[2,256,256]{2,1,0:T(8,128)}), f32[2,256,256]{2,1,0:T(8,128)}) %all-reduce.7.cloned.1.call-update) | async-done | bytes 524304 | tf_op jit(solution)/shard_map/psum | solution.py:83
  549.6 1.9 broadcast_multiply_fusion
  (39 shorter events, 3.6 us)
Async XLA Ops:
  7.2 3.8 copy-start.8
  7.2 4.5 copy-start.3
  7.2 542.4 %all-reduce.7.cloned.1.call-start = ((), (), s32[]{:S(2)}) async-start(), calls=%async_computation | async-start | bytes 1048576 | tf_op jit(solution)/shard_map/psum | solution.py:83
  8.3 18.1 %collective-permute-start.3 = (f32[1,256,256]{2,1,0:T(8,128)S(1)}, f32[1,256,256]{2,1,0:T(8,128)}, u32[]{:S(2)}, u32[]{:S(2)}) collective-permute-start(f32[1,256,256]{2,1,0:T(8,128)S(1)} %get-tuple-element.24), channel_id=1, source_target_pairs={{0,1},{1,2},{2,3},{3,4},{4,5},{5,6},{6,7},{7,8},{8,9},{9,10},{10,1... | collective-permute-start | bytes 786440 | tf_op jit(solution)/shard_map/ppermute | solution.py:19
  11.7 14.2 %copy-start = (f32[1,2,256,256]{3,2,1,0:T(8,128)S(1)}, f32[1,2,256,256]{3,2,1,0:T(8,128)}, u32[]{:S(2)}) copy-start(f32[1,2,256,256]{3,2,1,0:T(8,128)} %param.11) | copy-start | bytes 1572868
  14.7 11.7 %collective-permute-start.2 = (f32[1,256,256]{2,1,0:T(8,128)S(1)}, f32[1,256,256]{2,1,0:T(8,128)S(1)}, u32[]{:S(2)}, u32[]{:S(2)}) collective-permute-start(f32[1,256,256]{2,1,0:T(8,128)S(1)} %get-tuple-element.22), channel_id=1, source_target_pairs={{0,1},{1,2},{2,3},{3,4},{4,5},{5,6},{6,7},{7,8},{8,9},{9,10},{10,1... | collective-permute-start | bytes 786440 | tf_op jit(solution)/shard_map/ppermute | solution.py:19
  18.3 8.1 %collective-permute-start.1 = (f32[1,256,256]{2,1,0:T(8,128)S(1)}, f32[1,256,256]{2,1,0:T(8,128)S(1)}, u32[]{:S(2)}, u32[]{:S(2)}) collective-permute-start(f32[1,256,256]{2,1,0:T(8,128)S(1)} %get-tuple-element.23), channel_id=1, source_target_pairs={{1,0},{2,1},{3,2},{4,3},{5,4},{6,5},{7,6},{8,7},{9,8},{10,9},{11,1... | collective-permute-start | bytes 786440 | tf_op jit(solution)/shard_map/ppermute | solution.py:20
  20.3 9.5 %collective-permute-start = (f32[1,256,256]{2,1,0:T(8,128)S(1)}, f32[1,256,256]{2,1,0:T(8,128)S(1)}, u32[]{:S(2)}, u32[]{:S(2)}) collective-permute-start(f32[1,256,256]{2,1,0:T(8,128)S(1)} %get-tuple-element.21), channel_id=1, source_target_pairs={{1,0},{2,1},{3,2},{4,3},{5,4},{6,5},{7,6},{8,7},{9,8},{10,9},{11,1... | collective-permute-start | bytes 786440 | tf_op jit(solution)/shard_map/ppermute | solution.py:20
  29.7 2.6 copy-start.5
  218.3 7.7 %collective-permute-start.5 = (f32[1,256,256]{2,1,0:T(8,128)S(1)}, f32[1,256,256]{2,1,0:T(8,128)S(1)}, u32[]{:S(2)}, u32[]{:S(2)}) collective-permute-start(f32[1,256,256]{2,1,0:T(8,128)S(1)} %get-tuple-element.16), channel_id=1, source_target_pairs={{0,1},{1,2},{2,3},{3,4},{4,5},{5,6},{6,7},{7,8},{8,9},{9,10},{10,1... | collective-permute-start | bytes 786440 | tf_op jit(solution)/shard_map/ppermute | solution.py:19
  220.8 10.9 %copy-start.6 = (f32[1,256,256]{2,1,0:T(8,128)S(1)}, f32[1,256,256]{2,1,0:T(8,128)}, u32[]{:S(2)}) copy-start(f32[1,256,256]{2,1,0:T(8,128)} %copy-done.5) | copy-start | bytes 786436
  220.8 10.8 %collective-permute-start.4 = (f32[1,256,256]{2,1,0:T(8,128)S(1)}, f32[1,256,256]{2,1,0:T(8,128)S(1)}, u32[]{:S(2)}, u32[]{:S(2)}) collective-permute-start(f32[1,256,256]{2,1,0:T(8,128)S(1)} %get-tuple-element.15), channel_id=1, source_target_pairs={{1,0},{2,1},{3,2},{4,3},{5,4},{6,5},{7,6},{8,7},{9,8},{10,9},{11,1... | collective-permute-start | bytes 786440 | tf_op jit(solution)/shard_map/ppermute | solution.py:20
  233.2 91.1 %copy-start.2 = (f32[1,2,256,256]{3,2,1,0:T(8,128)S(1)}, f32[1,2,256,256]{3,2,1,0:T(8,128)}, u32[]{:S(2)}) copy-start(f32[1,2,256,256]{3,2,1,0:T(8,128)} %param.10) | copy-start | bytes 1572868
  324.2 16.7 %copy-start.1 = (f32[1,2,256,256]{3,2,1,0:T(8,128)}, f32[1,2,256,256]{3,2,1,0:T(8,128)S(1)}, u32[]{:S(2)}) copy-start(f32[1,2,256,256]{3,2,1,0:T(8,128)S(1)} %add_bitcast_fusion) | copy-start | bytes 1572868
  324.3 11.0 %collective-permute-start.7 = (f32[2,1,256,256]{3,2,1,0:T(8,128)S(1)}, f32[2,1,256,256]{3,2,1,0:T(8,128)S(1)}, u32[]{:S(2)}, u32[]{:S(2)}) collective-permute-start(f32[2,1,256,256]{3,2,1,0:T(8,128)S(1)} %get-tuple-element.10), channel_id=1, source_target_pairs={{0,1},{1,2},{2,3},{3,4},{4,5},{5,6},{6,7},{7,8},{8,9},{9,10},{10,1... | collective-permute-start | bytes 1572872 | tf_op jit(solution)/shard_map/ppermute | solution.py:19
  332.3 8.6 %collective-permute-start.6 = (f32[2,1,256,256]{3,2,1,0:T(8,128)S(1)}, f32[2,1,256,256]{3,2,1,0:T(8,128)S(1)}, u32[]{:S(2)}, u32[]{:S(2)}) collective-permute-start(f32[2,1,256,256]{3,2,1,0:T(8,128)S(1)} %get-tuple-element.9), channel_id=1, source_target_pairs={{1,0},{2,1},{3,2},{4,3},{5,4},{6,5},{7,6},{8,7},{9,8},{10,9},{11,1... | collective-permute-start | bytes 1572872 | tf_op jit(solution)/shard_map/ppermute | solution.py:20
  341.2 1.0 copy-start.4
  341.2 1.2 copy-start.7
Sparse Core Ops, SparseCore 0:
  346.5 203.0 all-reduce.6
where the time goes:
time: 559 us; the launch traced here: 558 us
  blocking collectives  272 us (49%)
  waiting for transfers between devices  220 us (39%)
  starting transfers between devices  28.7 us (5%)
  between operations  18.9 us (3%)
  other arithmetic  15.4 us (3%)
    psum x1, waiting for transfers between devices, local(): summed = lax.psum(contribution, 'pos')  203 us
    psum x2, blocking collectives, squares(): return lax.psum(jnp.sum(residual * residual), 'slab')  182 us
    psum x1, blocking collectives, local(): alpha = norm_now / lax.psum(jnp.sum(direction * image), 'slab')  89.6 us
    ppermute x4, starting transfers between devices, padded(): before = lax.ppermute(last, axis, up)  16 us
    ppermute x4, waiting for transfers between devices, padded(): after = lax.ppermute(first, axis, down)  14.6 us
    ppermute x4, starting transfers between devices, padded(): after = lax.ppermute(first, axis, down)  12.7 us
  transfers between devices with their start and end apart: 9, of which 5 were waited for; matrix products, arithmetic and copies ran while one was open for 1% of the time, Pallas kernels for 0%

commit v1 on v0

v1 whole, which is shorter than its diff:
```python
import jax
import jax.numpy as jnp
from jax import lax
from jax.experimental import pallas as pl
from jax.experimental.pallas import tpu as pltpu
from jax.sharding import PartitionSpec as P

MESH = pl.DeviceIdType.MESH
PAD = 8
ROWS = 32
diagonal_shift = 0.5


def fold(block):
    half = block.shape[1] // 2
    narrow = block[:, :half] + block[:, half:]
    return narrow.reshape(narrow.shape[0] // 8, 8, half).sum(axis=0)


def kernel(
    reluctivity, shift, labels, mask, potential, load, gradient, adjoint,
    label_x, nu_x, d_x, w_x, r_x, a_x, pot_x, mask_x, term, tile, near, far,
    part_x, part_z, piece, merged, local_sem, send_sem, recv_sem,
    near_send, near_recv, far_send, far_recv, x_send, x_recv, z_send, z_recv, out_sem,
):
    pos, slab = lax.axis_index("pos"), lax.axis_index("slab")
    n_slab = lax.axis_size("slab")
    up, down = lax.rem(slab + 1, n_slab), lax.rem(slab + n_slab - 1, n_slab)
    z_hi, inner = slab // 8, lax.rem(slab, 8)
    z_lo, x = pos // 4, lax.rem(pos, 4)
    cx, cy = labels.shape[1], labels.shape[2]

    local = [
        pltpu.make_async_copy(source, target, local_sem.at[i])
        for i, (source, target) in enumerate(
            (
                (load.at[0], d_x.at[pl.ds(1, 2), pl.ds(PAD, cx)]),
                (labels, label_x.at[pl.ds(1, 2)]),
                (potential.at[0], pot_x.at[pl.ds(1, 2), pl.ds(PAD, cx)]),
                (mask, mask_x),
            )
        )
    ]
    for copy in local:
        copy.start()

    def near_peer(o):
        return {"slab": z_hi * 8 + lax.rem(inner + o, 8)}

    def far_peer(o):
        return {"slab": lax.rem(z_hi + o, 4) * 8 + inner}

    def x_index(o):
        return lax.rem(x + o, 4)

    def z_index(o):
        return lax.rem(z_lo + o, 4)

    peers = [{"slab": up}, {"slab": down}]
    peers += [near_peer(o) for o in range(1, 8)]
    peers += [far_peer(o) for o in range(1, 4)]
    peers += [{"pos": z_lo * 4 + x_index(o)} for o in range(1, 4)]
    peers += [{"pos": z_index(o) * 4 + x} for o in range(1, 4)]
    barrier = pltpu.get_barrier_semaphore()
    for peer in peers:
        pl.semaphore_signal(barrier, inc=1, device_id=peer, device_id_type=MESH)
    pl.semaphore_wait(barrier, len(peers))

    def halo(which, first, last, target):
        return [
            pltpu.make_async_remote_copy(
                src_ref=source,
                dst_ref=target(ghost),
                send_sem=send_sem.at[2 * which + side],
                recv_sem=recv_sem.at[2 * which + side],
                device_id={"slab": peer},
                device_id_type=MESH,
            )
            for side, (source, ghost, peer) in enumerate(((last, 0, up), (first, 3, down)))
        ]

    def padded(ref):
        return lambda layer: ref.at[layer, pl.ds(PAD, cx)]

    d_halo = halo(0, load.at[0, 0], load.at[0, 1], padded(d_x))
    label_halo = halo(1, labels.at[0], labels.at[1], lambda layer: label_x.at[layer])
    pot_halo = halo(2, potential.at[0, 0], potential.at[0, 1], padded(pot_x))
    for copy in d_halo + label_halo + pot_halo:
        copy.start()

    for ref in (nu_x, d_x, r_x, a_x, pot_x):
        for layer in (1, 2):
            ref[layer, pl.ds(0, PAD), :] = jnp.zeros((PAD, cy), jnp.float32)
            ref[layer, pl.ds(PAD + cx, PAD), :] = jnp.zeros((PAD, cy), jnp.float32)

    low = jnp.where(slab > 0, 1.0, 0.0)
    high = jnp.where(slab < n_slab - 1, 1.0, 0.0)
    live = (low, 1.0, 1.0, high)
    table = [reluctivity[i] for i in range(4)]
    offset = shift[0]

    def materials(layers):
        def lookup(index):
            result = jnp.where(index == 1, table[1], table[0])
            result = jnp.where(index == 2, table[2], result)
            return jnp.where(index == 3, table[3], result)

        @pl.loop(0, cx // 2 // ROWS)
        def _(i):
            r = pl.multiple_of(i * ROWS, ROWS)
            s = pl.multiple_of(i * ROWS + cx // 2, ROWS)
            for layer in layers:
                turned = pltpu.roll(lookup(label_x[layer, pl.ds(r, ROWS), :]), offset, 1)
                nu_x[layer, pl.ds(PAD + r, ROWS), :] = turned * live[layer]
                still = lookup(label_x[layer, pl.ds(s, ROWS), :])
                nu_x[layer, pl.ds(PAD + s, ROWS), :] = still * live[layer]

    def at(ref, layer, r):
        return ref[layer, pl.ds(PAD + r, ROWS), :]

    def tall(ref, layer, r):
        return ref[layer, pl.ds(r, ROWS + 2 * PAD), :]

    def middle(block):
        return block[PAD : PAD + ROWS]

    def before(block):
        return pltpu.roll(block, 1, 0)

    def after(block):
        return pltpu.roll(block, ROWS + 2 * PAD - 1, 0)

    def operator(ref, layer, r, below, above):
        v_tall, nu_tall = tall(ref, layer, r), tall(nu_x, layer, r)
        flux = 0.5 * (nu_tall + after(nu_tall)) * (v_tall - after(v_tall))
        v, nu = middle(v_tall), middle(nu_tall)
        result = diagonal_shift * v + middle(flux - before(flux))
        for other_nu, other in ((at(nu_x, layer - 1, r), below), (at(nu_x, layer + 1, r), above)):
            result += 0.5 * (nu + other_nu) * (v - other)
        flux = 0.5 * (nu + pltpu.roll(nu, cy - 1, 1)) * (v - pltpu.roll(v, cy - 1, 1))
        return v, result + (flux - pltpu.roll(flux, 1, 1))

    zero = jnp.zeros((8, cy // 2), jnp.float32)

    local[1].wait()
    materials((1, 2))
    for copy in label_halo:
        copy.wait()
    materials((0, 3))
    local[0].wait()
    for copy in d_halo:
        copy.wait()

    def first_pass(i, sums):
        norm, energy = sums
        r = pl.multiple_of(i * ROWS, ROWS)
        edge = (at(d_x, 0, r) * low, at(d_x, 3, r) * high)
        for layer in (1, 2):
            below = edge[0] if layer == 1 else at(d_x, 1, r)
            above = edge[1] if layer == 2 else at(d_x, 2, r)
            v, image = operator(d_x, layer, r, below, above)
            w_x[layer, pl.ds(r, ROWS), :] = image
            norm += fold(v * v)
            energy += fold(v * image)
        return norm, energy

    sums = lax.fori_loop(0, cx // ROWS, first_pass, (zero, zero))

    w_halo = halo(3, w_x.at[1], w_x.at[2], lambda layer: w_x.at[layer])
    for copy in w_halo:
        copy.start()

    def reduce(which, parts):
        for i, part in enumerate(parts):
            tile[which, 0, pl.ds(i, 1), :] = jnp.sum(part, axis=0, keepdims=True)

        def exchange(stage, size, mine, box, peer, send, recv):
            copies = [
                pltpu.make_async_remote_copy(
                    src_ref=tile.at[which, stage],
                    dst_ref=box.at[which, mine],
                    send_sem=send.at[which, o - 1],
                    recv_sem=recv.at[which, o - 1],
                    device_id=peer(o),
                    device_id_type=MESH,
                )
                for o in range(1, size)
            ]
            for copy in copies:
                copy.start()
            box[which, mine] = tile[which, stage]
            for copy in copies:
                copy.wait()
            return sum((box[which, i] for i in range(1, size)), box[which, 0])

        tile[which, 1] = exchange(0, 8, inner, near, near_peer, near_send, near_recv)
        total = exchange(1, 4, z_hi, far, far_peer, far_send, far_recv)
        return [jnp.sum(total[i : i + 1, :], axis=1, keepdims=True) for i in range(len(parts))]

    rr0, energy0 = reduce(0, sums)
    alpha0 = rr0 / energy0
    for copy in w_halo:
        copy.wait()

    @pl.loop(0, cx // ROWS)
    def _(i):
        r = pl.multiple_of(i * ROWS, ROWS)
        for layer in range(4):
            rest = at(d_x, layer, r) - alpha0 * w_x[layer, pl.ds(r, ROWS), :]
            r_x[layer, pl.ds(PAD + r, ROWS), :] = rest * live[layer]

    def second_pass(i, sums):
        norm, energy, cross = sums
        r = pl.multiple_of(i * ROWS, ROWS)
        for layer in (1, 2):
            v, image = operator(r_x, layer, r, at(r_x, layer - 1, r), at(r_x, layer + 1, r))
            norm += fold(v * v)
            energy += fold(v * image)
            cross += fold(v * w_x[layer, pl.ds(r, ROWS), :])
        return norm, energy, cross

    sums = lax.fori_loop(0, cx // ROWS, second_pass, (zero, zero, zero))
    rr1, energy1, cross1 = reduce(1, sums)
    beta = rr1 / rr0
    alpha1 = rr1 / (energy1 + beta * (2.0 * cross1 + beta * energy0))
    scale = alpha0 + alpha1 * beta

    @pl.loop(0, cx // ROWS)
    def _(i):
        r = pl.multiple_of(i * ROWS, ROWS)
        for layer in range(4):
            value = scale * (at(d_x, layer, r) * live[layer]) + alpha1 * at(r_x, layer, r)
            a_x[layer, pl.ds(PAD + r, ROWS), :] = value

    finish = pltpu.make_async_copy(a_x.at[pl.ds(1, 2), pl.ds(PAD, cx)], adjoint.at[0], out_sem.at[0])
    finish.start()
    local[2].wait()
    local[3].wait()
    for copy in pot_halo:
        copy.wait()

    def slopes(ref, layer, r, below, above):
        v_tall = tall(ref, layer, r)
        v = middle(v_tall)
        return (
            above - below,
            middle(after(v_tall) - before(v_tall)),
            pltpu.roll(v, cy - 1, 1) - pltpu.roll(v, 1, 1),
        )

    @pl.loop(0, cx // ROWS)
    def _(i):
        r = pl.multiple_of(i * ROWS, ROWS)
        for layer in (1, 2):
            below, above = at(pot_x, layer - 1, r), at(pot_x, layer + 1, r)
            if layer == 1:
                below = below * low
            else:
                above = above * high
            pot = slopes(pot_x, layer, r, below, above)
            adj = slopes(a_x, layer, r, at(a_x, layer - 1, r), at(a_x, layer + 1, r))
            total = sum(p * (a + 0.5 * p) for p, a in zip(pot, adj))
            chosen = mask_x[layer - 1, pl.ds(r, ROWS), :].astype(jnp.float32)
            value = 0.25 * chosen * at(nu_x, layer, r) * total
            term[pl.ds((layer - 1) * cx + r, ROWS), :] = value

    quarter, small = 2 * cx // 4, 2 * cx // 16

    def scatter(mine, index, peer, source, size, box, send, recv):
        return [
            pltpu.make_async_remote_copy(
                src_ref=source.at[pl.ds(pl.multiple_of(index(o) * size, size), size)],
                dst_ref=box.at[o - 1],
                send_sem=send.at[0, o - 1],
                recv_sem=recv.at[0, o - 1],
                device_id=peer(o),
                device_id_type=MESH,
            )
            for o in range(1, 4)
        ]

    def x_peer(o):
        return {"pos": z_lo * 4 + x_index(o)}

    def z_peer(o):
        return {"pos": z_index(o) * 4 + x}

    copies = scatter(x, x_index, x_peer, term, quarter, part_x, x_send, x_recv)
    for copy in copies:
        copy.start()
    for copy in copies:
        copy.wait()

    @pl.loop(0, quarter // ROWS)
    def _(i):
        r = pl.multiple_of(i * ROWS, ROWS)
        own = term[pl.ds(pl.multiple_of(x * quarter + r, ROWS), ROWS), :]
        for o in range(3):
            own += part_x[o, pl.ds(r, ROWS), :]
        piece[pl.ds(r, ROWS), :] = own

    copies = scatter(z_lo, z_index, z_peer, piece, small, part_z, z_send, z_recv)
    for copy in copies:
        copy.start()
    for copy in copies:
        copy.wait()

    own_small = pl.ds(pl.multiple_of(x * quarter + z_lo * small, small), small)
    total = piece[pl.ds(pl.multiple_of(z_lo * small, small), small), :]
    for o in range(3):
        total += part_z[o]
    merged[own_small, :] = total / lax.axis_size("pos")

    def spread(where, peer, send, recv):
        return [
            pltpu.make_async_remote_copy(
                src_ref=merged.at[where],
                dst_ref=merged.at[where],
                send_sem=send.at[1, o - 1],
                recv_sem=recv.at[1, o - 1],
                device_id=peer(o),
                device_id_type=MESH,
            )
            for o in range(1, 4)
        ]

    copies = spread(own_small, z_peer, z_send, z_recv)
    for copy in copies:
        copy.start()
    for copy in copies:
        copy.wait()
    own_quarter = pl.ds(pl.multiple_of(x * quarter, quarter), quarter)
    copies = spread(own_quarter, x_peer, x_send, x_recv)
    for copy in copies:
        copy.start()
    for copy in copies:
        copy.wait()
    outs = [
        pltpu.make_async_copy(merged.at[pl.ds(layer * cx, cx)], gradient.at[layer], out_sem.at[1 + layer])
        for layer in range(2)
    ]
    for copy in outs:
        copy.start()
    for copy in outs:
        copy.wait()
    finish.wait()


def local(labels, magnet_mask, reluctivity, rotor_shift, potential, adjoint_load):
    cx, cy = labels.shape[1:]
    tall = cx + 2 * PAD
    floats = lambda *shape: pltpu.VMEM(shape, jnp.float32)
    sems = pltpu.SemaphoreType.DMA
    return pl.pallas_call(
        kernel,
        out_shape=(
            jax.ShapeDtypeStruct(labels.shape, jnp.float32),
            jax.ShapeDtypeStruct(adjoint_load.shape, jnp.float32),
        ),
        in_specs=[pl.BlockSpec(memory_space=pltpu.SMEM)] * 2 + [pl.BlockSpec(memory_space=pl.ANY)] * 4,
        out_specs=(pl.BlockSpec(memory_space=pl.ANY),) * 2,
        scratch_shapes=[
            pltpu.VMEM((4, cx, cy), jnp.int32),
            floats(4, tall, cy),
            floats(4, tall, cy),
            floats(4, cx, cy),
            floats(4, tall, cy),
            floats(4, tall, cy),
            floats(4, tall, cy),
            pltpu.VMEM((2, cx, cy), jnp.int32),
            floats(2 * cx, cy),
            floats(2, 2, 8, 128),
            floats(2, 8, 8, 128),
            floats(2, 4, 8, 128),
            floats(3, cx // 2, cy),
            floats(3, cx // 8, cy),
            floats(cx // 2, cy),
            floats(2 * cx, cy),
            sems((4,)),
            sems((8,)),
            sems((8,)),
            sems((2, 7)),
            sems((2, 7)),
            sems((2, 3)),
            sems((2, 3)),
            sems((2, 3)),
            sems((2, 3)),
            sems((2, 3)),
            sems((2, 3)),
            sems((3,)),
        ],
        compiler_params=pltpu.CompilerParams(
            collective_id=0, has_side_effects=True, vmem_limit_bytes=32 << 20
        ),
    )(reluctivity, rotor_shift, labels, magnet_mask, potential, adjoint_load)


def solution(mesh):
    return jax.shard_map(
        local,
        mesh=mesh,
        in_specs=(
            P("slab", None, None),
            P("slab", None, None),
            P(),
            P("pos"),
            P("pos", "slab", None, None),
            P("pos", "slab", None, None),
        ),
        out_specs=(P("slab", None, None), P("pos", "slab", None, None)),
        check_vma=False,
    )
```

time: 559 us -> 112 us (0.20)
  blocking collectives: 272 us -> 0 us
  waiting for transfers between devices: 220 us -> 0 us
  Pallas kernels: 0 us -> 105 us
  starting transfers between devices: 28.7 us -> 0 us
  between operations: 18.9 us -> 1.33 us
  other arithmetic: 15.4 us -> 0 us
    psum x3 -> x0, blocking collectives: 272 us -> none  [the longest x2 182 us: squares(): return lax.psum(jnp.sum(residual * residual), 'slab')]
    psum x1 -> x0, waiting for transfers between devices: 203 us -> none  [local(): summed = lax.psum(contribution, 'pos')]
    pallas_call x0 -> x1, Pallas kernels: none -> 105 us  [local(): pl.pallas_call(kernel, out_shape=(jax.ShapeDtypeStruct(labels.shape, jnp....]
    ppermute x8 -> x0, starting transfers between devices: 28.7 us -> none  [the longest x4 16 us: padded(): before = lax.ppermute(last, axis, up)]
    ppermute x8 -> x0, waiting for transfers between devices: 16.4 us -> none  [the longest x4 14.6 us: padded(): after = lax.ppermute(first, axis, down)]
  transfers between devices with their start and end apart: 9 -> 0, of which waited for: 5 -> 0; matrix products, arithmetic and copies ran while one was open for 1% -> 0% of each run, Pallas kernels for 0% -> 0%
where the time goes in v1:
time: 112 us
  Pallas kernels  105 us (94%)
  local copies, waits for them, and re-layouts  5.75 us (5%)
  between operations  1.33 us (1%)
    pallas_call x1, Pallas kernels, local(): pl.pallas_call(kernel, out_shape=(jax.ShapeDtypeStruct(labels.shape, jnp....  105 us
    unnamed x12, local copies, waits for them, and re-layouts  5.75 us

profile of v1, /device:TPU:8, one launch (start us, length us, event | category | flops | bytes accessed | tf_op | source)
XLA Modules:
  0.0 112.0 jit_solution(12642144501434550331)
XLA Ops:
  0.6 0.0 copy-start.4
  1.3 0.0 copy-done.4
  1.3 0.0 copy-start
  1.3 1.0 copy-done
  2.4 0.0 copy-start.1
  2.4 1.0 copy-done.1
  3.4 0.0 copy-start.2
  3.4 1.0 copy-done.2
  4.4 0.0 copy-start.3
  4.4 1.0 copy-done.3
  5.5 105.0 %shard_map.77 = (f32[2,256,256]{2,1,0:T(8,128)S(1)}, f32[1,2,256,256]{3,2,1,0:T(8,128)S(1)}) custom-call(f32[4]{0:T(128)S(1)} %copy-done.4, s32[1]{0:T(128)S(6)} %copy.10.shift, s32[2,256,256]{2,1,0:T(8,128)S(1)} %copy-done, s32[2,256,256]{2,1,0:T(8,128)S(1)} %copy-done.1, f32[1,2,256,256]{3,2,1,0:T(8,128)S(1)} %copy-done.2, f32[1,2,256,256]{3,2,1,0:T(8,128)S(1)} %copy-done.3), custom_call_target="tpu_custom_call" | custom-call | tf_op jit(solution)/shard_map/pallas_call | solution.py:354
  110.4 0.8 copy.11
  111.2 0.8 copy.12
Async XLA Ops:
  0.6 0.7 copy-start.4
  1.3 1.0 copy-start
  2.4 1.0 copy-start.1
  3.4 1.0 copy-start.2
  4.4 1.0 copy-start.3

commit v2 on v1

--- a/solution.py
+++ b/solution.py
@@ -19,8 +19,8 @@
 
 def kernel(
     reluctivity, shift, labels, mask, potential, load, gradient, adjoint,
-    label_x, nu_x, d_x, w_x, r_x, a_x, pot_x, mask_x, term, tile, near, far,
-    part_x, part_z, piece, merged, local_sem, send_sem, recv_sem,
+    label_x, nu_x, d_x, w_x, a_x, pot_x, mask_x, term, relay, relay_label, tile, near, far,
+    part_x, part_z, piece, merged, local_sem, send_sem, recv_sem, relay_send, relay_recv,
     near_send, near_recv, far_send, far_recv, x_send, x_recv, z_send, z_recv, out_sem,
 ):
     pos, slab = lax.axis_index("pos"), lax.axis_index("slab")
@@ -62,33 +62,161 @@
     peers += [{"pos": z_lo * 4 + x_index(o)} for o in range(1, 4)]
     peers += [{"pos": z_index(o) * 4 + x} for o in range(1, 4)]
     barrier = pltpu.get_barrier_semaphore()
+
+    def greet(peer):
+        pl.semaphore_signal(barrier, inc=1, device_id=peer, device_id_type=MESH)
+
+    z_up, z_down = lax.rem(z_hi + 1, 4) * 8, lax.rem(z_hi + 3, 4) * 8
+    is_first, is_last = inner == 0, inner == 7
+    odd = lax.rem(inner, 2) == 1
+    is_up_relay = jnp.logical_and(odd, inner < 7)
+    is_down_relay = jnp.logical_and(jnp.logical_not(odd), inner > 0)
     for peer in peers:
-        pl.semaphore_signal(barrier, inc=1, device_id=peer, device_id_type=MESH)
-    pl.semaphore_wait(barrier, len(peers))
-
-    def halo(which, first, last, target):
-        return [
-            pltpu.make_async_remote_copy(
-                src_ref=source,
-                dst_ref=target(ghost),
-                send_sem=send_sem.at[2 * which + side],
-                recv_sem=recv_sem.at[2 * which + side],
-                device_id={"slab": peer},
-                device_id_type=MESH,
-            )
-            for side, (source, ghost, peer) in enumerate(((last, 0, up), (first, 3, down)))
-        ]
+        greet(peer)
+
+    @pl.when(is_first)
+    def _():
+        for i in (1, 3, 5):
+            greet({"slab": z_down + i})
+
+    @pl.when(is_last)
+    def _():
+        for i in (2, 4, 6):
+            greet({"slab": z_up + i})
+
+    @pl.when(is_up_relay)
+    def _():
+        greet({"slab": z_up})
+
+    @pl.when(is_down_relay)
+    def _():
+        greet({"slab": z_down + 7})
+
+    ends = jnp.logical_or(is_first, is_last)
+    pl.semaphore_wait(barrier, len(peers) + jnp.where(ends, 3, 1))
+    strip = cx // 4
+    row = inner // 2
+
+    class Halo:
+        def __init__(self, which, first, last, target, buffer):
+            def send(source, where, peer, side, k):
+                return pltpu.make_async_remote_copy(
+                    src_ref=source,
+                    dst_ref=where,
+                    send_sem=send_sem.at[which, side, k],
+                    recv_sem=recv_sem.at[which, side, k],
+                    device_id={"slab": peer},
+                    device_id_type=MESH,
+                )
+
+            def through(source, k, peer):
+                return pltpu.make_async_remote_copy(
+                    src_ref=source.at[pl.ds(k * strip, strip)],
+                    dst_ref=buffer,
+                    send_sem=send_sem.at[which, 2, k],
+                    recv_sem=relay_recv.at[which],
+                    device_id={"slab": peer},
+                    device_id_type=MESH,
+                )
+
+            def forward(side, ghost, peer):
+                where = pl.ds(pl.multiple_of(row * strip, strip), strip)
+                return pltpu.make_async_remote_copy(
+                    src_ref=buffer,
+                    dst_ref=target(ghost).at[where],
+                    send_sem=relay_send.at[which],
+                    recv_sem=recv_sem.at[which, side, row],
+                    device_id={"slab": peer},
+                    device_id_type=MESH,
+                )
+
+            def pieces(source, side, ghost, peer):
+                return [
+                    send(
+                        source.at[pl.ds(k * strip, strip)],
+                        target(ghost).at[pl.ds(k * strip, strip)],
+                        peer, side, k,
+                    )
+                    for k in range(4)
+                ]
+
+            self.whole = [
+                (send(last, target(0), up, 0, 0), is_last, is_first),
+                (send(first, target(3), down, 1, 0), is_first, is_last),
+            ]
+            self.parts = [pieces(last, 0, 0, up), pieces(first, 1, 3, down)]
+            self.through = [
+                [through(last, k, z_hi * 8 + 2 * k + 1) for k in (0, 1, 2)],
+                [through(first, k, z_hi * 8 + 2 * k) for k in (1, 2, 3)],
+            ]
+            self.forward = [
+                (is_up_relay, forward(0, 0, z_up)),
+                (is_down_relay, forward(1, 3, z_down + 7)),
+            ]
+            self.arrive = through(last, 0, z_hi * 8)
+
+        def start(self):
+            for side, (copy, leaves, _) in enumerate(self.whole):
+                direct = self.parts[side][3 - 3 * side]
+
+                @pl.when(leaves)
+                def _():
+                    for piece in self.through[side]:
+                        piece.start()
+                    direct.start()
+
+                @pl.when(jnp.logical_not(leaves))
+                def _():
+                    copy.start()
+
+        def relay(self):
+            for role, copy in self.forward:
+
+                @pl.when(role)
+                def _():
+                    self.arrive.wait_recv()
+                    copy.start()
+
+        def wait(self):
+            for side, (copy, leaves, enters) in enumerate(self.whole):
+                direct = self.parts[side][3 - 3 * side]
+
+                @pl.when(enters)
+                def _():
+                    for piece in self.parts[side]:
+                        piece.wait_recv()
+
+                @pl.when(jnp.logical_not(enters))
+                def _():
+                    copy.wait_recv()
+
+                @pl.when(leaves)
+                def _():
+                    for piece in self.through[side]:
+                        piece.wait_send()
+                    direct.wait_send()
+
+                @pl.when(jnp.logical_not(leaves))
+                def _():
+                    copy.wait_send()
+
+            for role, copy in self.forward:
+
+                @pl.when(role)
+                def _():
+                    copy.wait_send()
 
     def padded(ref):
         return lambda layer: ref.at[layer, pl.ds(PAD, cx)]
 
-    d_halo = halo(0, load.at[0, 0], load.at[0, 1], padded(d_x))
-    label_halo = halo(1, labels.at[0], labels.at[1], lambda layer: label_x.at[layer])
-    pot_halo = halo(2, potential.at[0, 0], potential.at[0, 1], padded(pot_x))
-    for copy in d_halo + label_halo + pot_halo:
-        copy.start()
-
-    for ref in (nu_x, d_x, r_x, a_x, pot_x):
+    d_halo = Halo(0, load.at[0, 0], load.at[0, 1], padded(d_x), relay.at[0])
+    label_halo = Halo(1, labels.at[0], labels.at[1], lambda layer: label_x.at[layer], relay_label)
+    pot_halo = Halo(2, potential.at[0, 0], potential.at[0, 1], padded(pot_x), relay.at[1])
+    w_halo = Halo(3, padded(w_x)(1), padded(w_x)(2), padded(w_x), relay.at[2])
+    label_halo.start()
+    d_halo.start()
+
+    for ref in (nu_x, d_x, w_x, a_x, pot_x):
         for layer in (1, 2):
             ref[layer, pl.ds(0, PAD), :] = jnp.zeros((PAD, cy), jnp.float32)
             ref[layer, pl.ds(PAD + cx, PAD), :] = jnp.zeros((PAD, cy), jnp.float32)
@@ -144,100 +272,122 @@
 
     local[1].wait()
     materials((1, 2))
-    for copy in label_halo:
-        copy.wait()
+    label_halo.relay()
+    d_halo.relay()
+    label_halo.wait()
     materials((0, 3))
     local[0].wait()
-    for copy in d_halo:
-        copy.wait()
+    d_halo.wait()
+
+    def sides(ref, layer, r):
+        below, above = at(ref, layer - 1, r), at(ref, layer + 1, r)
+        return (below * low, above) if layer == 1 else (below, above * high)
 
     def first_pass(i, sums):
         norm, energy = sums
         r = pl.multiple_of(i * ROWS, ROWS)
-        edge = (at(d_x, 0, r) * low, at(d_x, 3, r) * high)
         for layer in (1, 2):
-            below = edge[0] if layer == 1 else at(d_x, 1, r)
-            above = edge[1] if layer == 2 else at(d_x, 2, r)
-            v, image = operator(d_x, layer, r, below, above)
-            w_x[layer, pl.ds(r, ROWS), :] = image
+            v, image = operator(d_x, layer, r, *sides(d_x, layer, r))
+            w_x[layer, pl.ds(PAD + r, ROWS), :] = image
             norm += fold(v * v)
             energy += fold(v * image)
         return norm, energy
 
     sums = lax.fori_loop(0, cx // ROWS, first_pass, (zero, zero))
-
-    w_halo = halo(3, w_x.at[1], w_x.at[2], lambda layer: w_x.at[layer])
-    for copy in w_halo:
-        copy.start()
-
-    def reduce(which, parts):
-        for i, part in enumerate(parts):
-            tile[which, 0, pl.ds(i, 1), :] = jnp.sum(part, axis=0, keepdims=True)
-
-        def exchange(stage, size, mine, box, peer, send, recv):
-            copies = [
-                pltpu.make_async_remote_copy(
-                    src_ref=tile.at[which, stage],
-                    dst_ref=box.at[which, mine],
-                    send_sem=send.at[which, o - 1],
-                    recv_sem=recv.at[which, o - 1],
-                    device_id=peer(o),
-                    device_id_type=MESH,
-                )
-                for o in range(1, size)
-            ]
-            for copy in copies:
-                copy.start()
-            box[which, mine] = tile[which, stage]
-            for copy in copies:
-                copy.wait()
-            return sum((box[which, i] for i in range(1, size)), box[which, 0])
-
-        tile[which, 1] = exchange(0, 8, inner, near, near_peer, near_send, near_recv)
-        total = exchange(1, 4, z_hi, far, far_peer, far_send, far_recv)
-        return [jnp.sum(total[i : i + 1, :], axis=1, keepdims=True) for i in range(len(parts))]
-
-    rr0, energy0 = reduce(0, sums)
-    alpha0 = rr0 / energy0
-    for copy in w_halo:
-        copy.wait()
+    w_halo.start()
+
+    def whole_sum(part):
+        return jnp.sum(jnp.sum(part, axis=0, keepdims=True), axis=1, keepdims=True)
+
+    def wide(value, width=cy):
+        return jnp.broadcast_to(value[:, :1], (1, width))
+
+    def quotient(top, bottom):
+        some = bottom > 0.0
+        return jnp.where(some, top / jnp.where(some, bottom, 1.0), 0.0)
+
+    norm, energy = [whole_sum(part) for part in sums]
+    theta = quotient(energy, norm)
+    theta_wide = wide(theta)
+    w_halo.relay()
+    w_halo.wait()
+    pot_halo.start()
+
+    def second_pass(i, sums):
+        m1, m2, m3, m4 = sums
+        r = pl.multiple_of(i * ROWS, ROWS)
+        for layer in (1, 2):
+            w, image = operator(w_x, layer, r, *sides(w_x, layer, r))
+            d = at(d_x, layer, r)
+            u = w - theta_wide * d
+            q = image - theta_wide * w
+            m1 += fold(d * u)
+            m2 += fold(u * u)
+            m3 += fold(u * q)
+            m4 += fold(d * q)
+        return m1, m2, m3, m4
+
+    sums = lax.fori_loop(0, cx // ROWS, second_pass, (zero,) * 4)
+
+    def combine(box):
+        th, m0, m1, m2, m3, m4 = [box[:, i, :] for i in range(6)]
+        total = lambda value: jnp.sum(value, axis=0, keepdims=True)
+        centre = quotient(total(th * m0 + m1), total(m0))
+        e = centre - th
+        dw = m1 + th * m0
+        return (
+            centre,
+            total(m0),
+            total(m1 - e * m0),
+            total(m2 - e * (2.0 * m1 - e * m0)),
+            total(m3 - e * (m2 + th * m1 + m4 - e * dw)),
+            total(m4 - e * dw),
+        )
+
+    def exchange(stage, values, size, mine, box, peer, send, recv):
+        for i, value in enumerate(values):
+            tile[stage, pl.ds(i, 1), :] = wide(value, tile.shape[2])
+        copies = [
+            pltpu.make_async_remote_copy(
+                src_ref=tile.at[stage],
+                dst_ref=box.at[mine],
+                send_sem=send.at[o - 1],
+                recv_sem=recv.at[o - 1],
+                device_id=peer(o),
+                device_id_type=MESH,
+            )
+            for o in range(1, size)
+        ]
+        for copy in copies:
+            copy.start()
+        box[mine] = tile[stage]
+        for copy in copies:
+            copy.wait()
+        return combine(box)
+
+    values = (theta, norm, *[whole_sum(part) for part in sums])
+    values = exchange(0, values, 8, inner, near, near_peer, near_send, near_recv)
+    pot_halo.relay()
+    values = exchange(1, values, 4, z_hi, far, far_peer, far_send, far_recv)
+    centre, m0, _, m2, m3, _ = values
+    alpha0 = 1.0 / centre
+    beta = alpha0 * alpha0 * m2 / m0
+    alpha1 = m2 / (m3 - alpha0 * m2 * (m2 / m0))
+    from_d = wide(alpha0 + alpha1 * (1.0 + beta))
+    from_w = wide(alpha0 * alpha1)
 
     @pl.loop(0, cx // ROWS)
     def _(i):
         r = pl.multiple_of(i * ROWS, ROWS)
         for layer in range(4):
-            rest = at(d_x, layer, r) - alpha0 * w_x[layer, pl.ds(r, ROWS), :]
-            r_x[layer, pl.ds(PAD + r, ROWS), :] = rest * live[layer]
-
-    def second_pass(i, sums):
-        norm, energy, cross = sums
-        r = pl.multiple_of(i * ROWS, ROWS)
-        for layer in (1, 2):
-            v, image = operator(r_x, layer, r, at(r_x, layer - 1, r), at(r_x, layer + 1, r))
-            norm += fold(v * v)
-            energy += fold(v * image)
-            cross += fold(v * w_x[layer, pl.ds(r, ROWS), :])
-        return norm, energy, cross
-
-    sums = lax.fori_loop(0, cx // ROWS, second_pass, (zero, zero, zero))
-    rr1, energy1, cross1 = reduce(1, sums)
-    beta = rr1 / rr0
-    alpha1 = rr1 / (energy1 + beta * (2.0 * cross1 + beta * energy0))
-    scale = alpha0 + alpha1 * beta
-
-    @pl.loop(0, cx // ROWS)
-    def _(i):
-        r = pl.multiple_of(i * ROWS, ROWS)
-        for layer in range(4):
-            value = scale * (at(d_x, layer, r) * live[layer]) + alpha1 * at(r_x, layer, r)
-            a_x[layer, pl.ds(PAD + r, ROWS), :] = value
+            value = from_d * at(d_x, layer, r) - from_w * at(w_x, layer, r)
+            a_x[layer, pl.ds(PAD + r, ROWS), :] = value * live[layer]
 
     finish = pltpu.make_async_copy(a_x.at[pl.ds(1, 2), pl.ds(PAD, cx)], adjoint.at[0], out_sem.at[0])
     finish.start()
     local[2].wait()
     local[3].wait()
-    for copy in pot_halo:
-        copy.wait()
+    pot_halo.wait()
 
     def slopes(ref, layer, r, below, above):
         v_tall = tall(ref, layer, r)
@@ -252,12 +402,7 @@
     def _(i):
         r = pl.multiple_of(i * ROWS, ROWS)
         for layer in (1, 2):
-            below, above = at(pot_x, layer - 1, r), at(pot_x, layer + 1, r)
-            if layer == 1:
-                below = below * low
-            else:
-                above = above * high
-            pot = slopes(pot_x, layer, r, below, above)
+            pot = slopes(pot_x, layer, r, *sides(pot_x, layer, r))
             adj = slopes(a_x, layer, r, at(a_x, layer - 1, r), at(a_x, layer + 1, r))
             total = sum(p * (a + 0.5 * p) for p, a in zip(pot, adj))
             chosen = mask_x[layer - 1, pl.ds(r, ROWS), :].astype(jnp.float32)
@@ -363,26 +508,29 @@
             pltpu.VMEM((4, cx, cy), jnp.int32),
             floats(4, tall, cy),
             floats(4, tall, cy),
-            floats(4, cx, cy),
             floats(4, tall, cy),
             floats(4, tall, cy),
             floats(4, tall, cy),
             pltpu.VMEM((2, cx, cy), jnp.int32),
             floats(2 * cx, cy),
-            floats(2, 2, 8, 128),
-            floats(2, 8, 8, 128),
-            floats(2, 4, 8, 128),
+            floats(3, cx // 4, cy),
+            pltpu.VMEM((cx // 4, cy), jnp.int32),
+            floats(2, 8, 128),
+            floats(8, 8, 128),
+            floats(4, 8, 128),
             floats(3, cx // 2, cy),
             floats(3, cx // 8, cy),
             floats(cx // 2, cy),
             floats(2 * cx, cy),
             sems((4,)),
-            sems((8,)),
-            sems((8,)),
-            sems((2, 7)),
-            sems((2, 7)),
-            sems((2, 3)),
-            sems((2, 3)),
+            sems((4, 3, 4)),
+            sems((4, 2, 4)),
+            sems((4,)),
+            sems((4,)),
+            sems((7,)),
+            sems((7,)),
+            sems((3,)),
+            sems((3,)),
             sems((2, 3)),
             sems((2, 3)),
             sems((2, 3)),
@@ -390,7 +538,7 @@
             sems((3,)),
         ],
         compiler_params=pltpu.CompilerParams(
-            collective_id=0, has_side_effects=True, vmem_limit_bytes=32 << 20
+            collective_id=0, has_side_effects=True, vmem_limit_bytes=60 << 20
         ),
     )(reluctivity, rotor_shift, labels, magnet_mask, potential, adjoint_load)
 

time: 112 us -> 86.4 us (0.77)
  the two profiles are of different devices: /device:TPU:8 before, /device:TPU:24 now
where the time goes in v2:
time: 86.4 us; the launch traced here: 86.2 us
  Pallas kernels  82.2 us (95%)
  local copies, waits for them, and re-layouts  2.72 us (3%)
  between operations  1.29 us (1%)
    pallas_call x1, Pallas kernels, local(): pl.pallas_call(kernel, out_shape=(jax.ShapeDtypeStruct(labels.shape, jnp....  82.2 us
    unnamed x4, local copies, waits for them, and re-layouts  2.72 us

profile of v2, /device:TPU:24, one launch (start us, length us, event | category | flops | bytes accessed | tf_op | source)
XLA Modules:
  0.0 86.2 jit_solution(1742629706804978331)
XLA Ops:
  1.3 82.2 %shard_map.77 = (f32[2,256,256]{2,1,0:T(8,128)}, f32[1,2,256,256]{3,2,1,0:T(8,128)}) custom-call(f32[4]{0:T(128)} %reluctivity.1, s32[1]{0:T(128)S(6)} %copy.10.shift, s32[2,256,256]{2,1,0:T(8,128)} %labels.1, s32[2,256,256]{2,1,0:T(8,128)} %mask.1, f32[1,2,256,256]{3,2,1,0:T(8,128)} %potential.1, f32[1,2,256,256]{3,2,1,0:T(8,128)} %load.1), custom_call_target="tpu_custom_call" | custom-call | tf_op jit(solution)/shard_map/pallas_call | solution.py:499
  83.5 0.0 copy-start
  83.5 1.9 %copy.11 = f32[2,256,256]{2,1,0:T(8,128)} copy(f32[2,256,256]{2,1,0:T(8,128)} %get-tuple-element.4) | data formatting | bytes 1048576
  85.4 0.0 copy-done
  85.4 0.8 copy.12
Async XLA Ops:
  83.5 1.9 %copy-start = (f32[1,2,256,256]{3,2,1,0:T(8,128)S(1)}, f32[1,2,256,256]{3,2,1,0:T(8,128)}, u32[]{:S(2)}) copy-start(f32[1,2,256,256]{3,2,1,0:T(8,128)} %get-tuple-element.5) | copy-start | bytes 1572868

commit v3 on v2

--- a/solution.py
+++ b/solution.py
@@ -94,8 +94,13 @@
 
     ends = jnp.logical_or(is_first, is_last)
     pl.semaphore_wait(barrier, len(peers) + jnp.where(ends, 3, 1))
-    strip = cx // 4
+    strip = cx * 7 // 32
     row = inner // 2
+
+    def part(side, k):
+        if k == 3 - 3 * side:
+            return pl.ds(0 if side else 3 * strip, cx - 3 * strip)
+        return pl.ds(k * strip + side * (cx - 4 * strip), strip)
 
     class Halo:
         def __init__(self, which, first, last, target, buffer):
@@ -109,9 +114,9 @@
                     device_id_type=MESH,
                 )
 
-            def through(source, k, peer):
+            def through(source, side, k, peer):
                 return pltpu.make_async_remote_copy(
-                    src_ref=source.at[pl.ds(k * strip, strip)],
+                    src_ref=source.at[part(side, k)],
                     dst_ref=buffer,
                     send_sem=send_sem.at[which, 2, k],
                     recv_sem=relay_recv.at[which],
@@ -120,7 +125,8 @@
                 )
 
             def forward(side, ghost, peer):
-                where = pl.ds(pl.multiple_of(row * strip, strip), strip)
+                first = row * strip + side * (cx - 4 * strip)
+                where = pl.ds(pl.multiple_of(first, PAD), strip)
                 return pltpu.make_async_remote_copy(
                     src_ref=buffer,
                     dst_ref=target(ghost).at[where],
@@ -133,8 +139,8 @@
             def pieces(source, side, ghost, peer):
                 return [
                     send(
-                        source.at[pl.ds(k * strip, strip)],
-                        target(ghost).at[pl.ds(k * strip, strip)],
+                        source.at[part(side, k)],
+                        target(ghost).at[part(side, k)],
                         peer, side, k,
                     )
                     for k in range(4)
@@ -146,14 +152,14 @@
             ]
             self.parts = [pieces(last, 0, 0, up), pieces(first, 1, 3, down)]
             self.through = [
-                [through(last, k, z_hi * 8 + 2 * k + 1) for k in (0, 1, 2)],
-                [through(first, k, z_hi * 8 + 2 * k) for k in (1, 2, 3)],
+                [through(last, 0, k, z_hi * 8 + 2 * k + 1) for k in (0, 1, 2)],
+                [through(first, 1, k, z_hi * 8 + 2 * k) for k in (1, 2, 3)],
             ]
             self.forward = [
                 (is_up_relay, forward(0, 0, z_up)),
                 (is_down_relay, forward(1, 3, z_down + 7)),
             ]
-            self.arrive = through(last, 0, z_hi * 8)
+            self.arrive = through(last, 0, 0, z_hi * 8)
 
         def start(self):
             for side, (copy, leaves, _) in enumerate(self.whole):
@@ -263,8 +269,9 @@
         flux = 0.5 * (nu_tall + after(nu_tall)) * (v_tall - after(v_tall))
         v, nu = middle(v_tall), middle(nu_tall)
         result = diagonal_shift * v + middle(flux - before(flux))
-        for other_nu, other in ((at(nu_x, layer - 1, r), below), (at(nu_x, layer + 1, r), above)):
-            result += 0.5 * (nu + other_nu) * (v - other)
+        for step, other in ((-1, below), (1, above)):
+            if other is not None:
+                result += 0.5 * (nu + at(nu_x, layer + step, r)) * (v - other)
         flux = 0.5 * (nu + pltpu.roll(nu, cy - 1, 1)) * (v - pltpu.roll(v, cy - 1, 1))
         return v, result + (flux - pltpu.roll(flux, 1, 1))
 
@@ -272,12 +279,24 @@
 
     local[1].wait()
     materials((1, 2))
+    local[0].wait()
+
+    @pl.loop(0, cx // ROWS)
+    def _(i):
+        r = pl.multiple_of(i * ROWS, ROWS)
+        for layer, others in ((1, (None, at(d_x, 2, r))), (2, (at(d_x, 1, r), None))):
+            _, image = operator(d_x, layer, r, *others)
+            w_x[layer, pl.ds(PAD + r, ROWS), :] = image
+
+    w_halo.start()
     label_halo.relay()
     d_halo.relay()
+    w_halo.relay()
     label_halo.wait()
     materials((0, 3))
-    local[0].wait()
     d_halo.wait()
+    w_halo.wait()
+    pot_halo.start()
 
     def sides(ref, layer, r):
         below, above = at(ref, layer - 1, r), at(ref, layer + 1, r)
@@ -286,15 +305,18 @@
     def first_pass(i, sums):
         norm, energy = sums
         r = pl.multiple_of(i * ROWS, ROWS)
-        for layer in (1, 2):
-            v, image = operator(d_x, layer, r, *sides(d_x, layer, r))
+        for layer, ghost, exists in ((1, 0, low), (2, 3, high)):
+            d = at(d_x, layer, r)
+            nu = at(nu_x, layer, r) + at(nu_x, ghost, r)
+            flux = 0.5 * nu * (d - at(d_x, ghost, r) * exists)
+            image = at(w_x, layer, r) + flux
             w_x[layer, pl.ds(PAD + r, ROWS), :] = image
-            norm += fold(v * v)
-            energy += fold(v * image)
+            w_x[ghost, pl.ds(PAD + r, ROWS), :] = at(w_x, ghost, r) - flux
+            norm += fold(d * d)
+            energy += fold(d * image)
         return norm, energy
 
     sums = lax.fori_loop(0, cx // ROWS, first_pass, (zero, zero))
-    w_halo.start()
 
     def whole_sum(part):
         return jnp.sum(jnp.sum(part, axis=0, keepdims=True), axis=1, keepdims=True)
@@ -309,10 +331,6 @@
     norm, energy = [whole_sum(part) for part in sums]
     theta = quotient(energy, norm)
     theta_wide = wide(theta)
-    w_halo.relay()
-    w_halo.wait()
-    pot_halo.start()
-
     def second_pass(i, sums):
         m1, m2, m3, m4 = sums
         r = pl.multiple_of(i * ROWS, ROWS)
@@ -513,8 +531,8 @@
             floats(4, tall, cy),
             pltpu.VMEM((2, cx, cy), jnp.int32),
             floats(2 * cx, cy),
-            floats(3, cx // 4, cy),
-            pltpu.VMEM((cx // 4, cy), jnp.int32),
+            floats(3, cx * 7 // 32, cy),
+            pltpu.VMEM((cx * 7 // 32, cy), jnp.int32),
             floats(2, 8, 128),
             floats(8, 8, 128),
             floats(4, 8, 128),

time: 86.4 us -> 76.9 us (0.89)
  the two profiles are of different devices: /device:TPU:24 before, /device:TPU:4 now
where the time goes in v3:
time: 76.9 us; the launch traced here: 76.8 us
  Pallas kernels  72.8 us (95%)
  local copies, waits for them, and re-layouts  2.72 us (4%)
  between operations  1.29 us (2%)
    pallas_call x1, Pallas kernels, local(): pl.pallas_call(kernel, out_shape=(jax.ShapeDtypeStruct(labels.shape, jnp....  72.8 us
    unnamed x4, local copies, waits for them, and re-layouts  2.72 us

profile of v3, /device:TPU:4, one launch (start us, length us, event | category | flops | bytes accessed | tf_op | source)
XLA Modules:
  0.0 76.8 jit_solution(3375937071409652085)
XLA Ops:
  1.3 72.8 %shard_map.77 = (f32[2,256,256]{2,1,0:T(8,128)}, f32[1,2,256,256]{3,2,1,0:T(8,128)}) custom-call(f32[4]{0:T(128)} %reluctivity.1, s32[1]{0:T(128)S(6)} %copy.10.shift, s32[2,256,256]{2,1,0:T(8,128)} %labels.1, s32[2,256,256]{2,1,0:T(8,128)} %mask.1, f32[1,2,256,256]{3,2,1,0:T(8,128)} %potential.1, f32[1,2,256,256]{3,2,1,0:T(8,128)} %load.1), custom_call_target="tpu_custom_call" | custom-call | tf_op jit(solution)/shard_map/pallas_call | solution.py:517
  74.1 0.0 copy-start
  74.1 1.9 %copy.11 = f32[2,256,256]{2,1,0:T(8,128)} copy(f32[2,256,256]{2,1,0:T(8,128)} %get-tuple-element.4) | data formatting | bytes 1048576
  76.0 0.0 copy-done
  76.0 0.8 %copy.12 = f32[1,2,256,256]{3,2,1,0:T(8,128)} copy(f32[1,2,256,256]{3,2,1,0:T(8,128)S(1)} %copy-done) | data formatting | bytes 1048576
Async XLA Ops:
  74.1 1.9 %copy-start = (f32[1,2,256,256]{3,2,1,0:T(8,128)S(1)}, f32[1,2,256,256]{3,2,1,0:T(8,128)}, u32[]{:S(2)}) copy-start(f32[1,2,256,256]{3,2,1,0:T(8,128)} %get-tuple-element.5) | copy-start | bytes 1572868

commit v4 on v3

--- a/solution.py
+++ b/solution.py
@@ -19,8 +19,8 @@
 
 def kernel(
     reluctivity, shift, labels, mask, potential, load, gradient, adjoint,
-    label_x, nu_x, d_x, w_x, a_x, pot_x, mask_x, term, relay, relay_label, tile, near, far,
-    part_x, part_z, piece, merged, local_sem, send_sem, recv_sem, relay_send, relay_recv,
+    label_x, nu_x, d_x, w_x, a_x, pot_x, mask_x, term, relay, tile, near, far,
+    part_x, part_z, piece, merged, local_sem, send_sem, recv_sem, relay_send, relay_recv, share_send, share_recv,
     near_send, near_recv, far_send, far_recv, x_send, x_recv, z_send, z_recv, out_sem,
 ):
     pos, slab = lax.axis_index("pos"), lax.axis_index("slab")
@@ -94,7 +94,7 @@
 
     ends = jnp.logical_or(is_first, is_last)
     pl.semaphore_wait(barrier, len(peers) + jnp.where(ends, 3, 1))
-    strip = cx * 7 // 32
+    strip = cx // 4
     row = inner // 2
 
     def part(side, k):
@@ -212,11 +212,88 @@
                 def _():
                     copy.wait_send()
 
+    class Shared:
+        def __init__(self, which, first, last, target):
+            def send(source, where, peer, side):
+                return pltpu.make_async_remote_copy(
+                    src_ref=source,
+                    dst_ref=where,
+                    send_sem=send_sem.at[which, side, 0],
+                    recv_sem=recv_sem.at[which, side, 0],
+                    device_id={"slab": peer},
+                    device_id_type=MESH,
+                )
+
+            quarter = pl.ds(pl.multiple_of(x * strip, strip), strip)
+
+            def share(ghost, o):
+                return pltpu.make_async_remote_copy(
+                    src_ref=target(ghost).at[quarter],
+                    dst_ref=target(ghost).at[quarter],
+                    send_sem=share_send.at[o - 1],
+                    recv_sem=share_recv.at[o - 1],
+                    device_id={"pos": z_lo * 4 + x_index(o)},
+                    device_id_type=MESH,
+                )
+
+            self.sides = [
+                (
+                    send(source, target(ghost), peer, side),
+                    send(source.at[quarter], target(ghost).at[quarter], peer, side),
+                    [share(ghost, o) for o in range(1, 4)],
+                    leaves,
+                    enters,
+                )
+                for side, (source, ghost, peer, leaves, enters) in enumerate(
+                    ((last, 0, up, is_last, is_first), (first, 3, down, is_first, is_last))
+                )
+            ]
+
+        def start(self):
+            for whole, quarter, _, leaves, _ in self.sides:
+
+                @pl.when(leaves)
+                def _():
+                    quarter.start()
+
+                @pl.when(jnp.logical_not(leaves))
+                def _():
+                    whole.start()
+
+        def relay(self):
+            for _, quarter, shares, _, enters in self.sides:
+
+                @pl.when(enters)
+                def _():
+                    quarter.wait_recv()
+                    for share in shares:
+                        share.start()
+
+        def wait(self):
+            for whole, quarter, shares, leaves, enters in self.sides:
+
+                @pl.when(enters)
+                def _():
+                    for share in shares:
+                        share.wait()
+
+                @pl.when(jnp.logical_not(enters))
+                def _():
+                    whole.wait_recv()
+
+                @pl.when(leaves)
+                def _():
+                    quarter.wait_send()
+
+                @pl.when(jnp.logical_not(leaves))
+                def _():
+                    whole.wait_send()
+
     def padded(ref):
         return lambda layer: ref.at[layer, pl.ds(PAD, cx)]
 
     d_halo = Halo(0, load.at[0, 0], load.at[0, 1], padded(d_x), relay.at[0])
-    label_halo = Halo(1, labels.at[0], labels.at[1], lambda layer: label_x.at[layer], relay_label)
+    label_halo = Shared(1, labels.at[0], labels.at[1], lambda layer: label_x.at[layer])
     pot_halo = Halo(2, potential.at[0, 0], potential.at[0, 1], padded(pot_x), relay.at[1])
     w_halo = Halo(3, padded(w_x)(1), padded(w_x)(2), padded(w_x), relay.at[2])
     label_halo.start()
@@ -468,17 +545,18 @@
     for copy in copies:
         copy.wait()
 
-    own_small = pl.ds(pl.multiple_of(x * quarter + z_lo * small, small), small)
-    total = piece[pl.ds(pl.multiple_of(z_lo * small, small), small), :]
+    own_small = pl.ds(pl.multiple_of(z_lo * small, small), small)
+    total = piece[own_small, :]
     for o in range(3):
         total += part_z[o]
     merged[own_small, :] = total / lax.axis_size("pos")
-
-    def spread(where, peer, send, recv):
-        return [
+    own_quarter = gradient.at[x // 2, pl.ds(pl.multiple_of(lax.rem(x, 2) * quarter, quarter), quarter)]
+
+    def spread(source, target, peer, send, recv):
+        copies = [
             pltpu.make_async_remote_copy(
-                src_ref=merged.at[where],
-                dst_ref=merged.at[where],
+                src_ref=source,
+                dst_ref=target,
                 send_sem=send.at[1, o - 1],
                 recv_sem=recv.at[1, o - 1],
                 device_id=peer(o),
@@ -486,26 +564,18 @@
             )
             for o in range(1, 4)
         ]
-
-    copies = spread(own_small, z_peer, z_send, z_recv)
-    for copy in copies:
-        copy.start()
+        for copy in copies:
+            copy.start()
+        return copies
+
+    for copy in spread(merged.at[own_small], merged.at[own_small], z_peer, z_send, z_recv):
+        copy.wait()
+    copies = spread(merged, own_quarter, x_peer, x_send, x_recv)
+    keep = pltpu.make_async_copy(merged, own_quarter, out_sem.at[1])
+    keep.start()
     for copy in copies:
         copy.wait()
-    own_quarter = pl.ds(pl.multiple_of(x * quarter, quarter), quarter)
-    copies = spread(own_quarter, x_peer, x_send, x_recv)
-    for copy in copies:
-        copy.start()
-    for copy in copies:
-        copy.wait()
-    outs = [
-        pltpu.make_async_copy(merged.at[pl.ds(layer * cx, cx)], gradient.at[layer], out_sem.at[1 + layer])
-        for layer in range(2)
-    ]
-    for copy in outs:
-        copy.start()
-    for copy in outs:
-        copy.wait()
+    keep.wait()
     finish.wait()
 
 
@@ -520,7 +590,7 @@
             jax.ShapeDtypeStruct(labels.shape, jnp.float32),
             jax.ShapeDtypeStruct(adjoint_load.shape, jnp.float32),
         ),
-        in_specs=[pl.BlockSpec(memory_space=pltpu.SMEM)] * 2 + [pl.BlockSpec(memory_space=pl.ANY)] * 4,
+        in_specs=[pl.BlockSpec(memory_space=pltpu.SMEM)] * 2 + [pl.BlockSpec(memory_space=pltpu.HBM)] * 4,
         out_specs=(pl.BlockSpec(memory_space=pl.ANY),) * 2,
         scratch_shapes=[
             pltpu.VMEM((4, cx, cy), jnp.int32),
@@ -531,20 +601,21 @@
             floats(4, tall, cy),
             pltpu.VMEM((2, cx, cy), jnp.int32),
             floats(2 * cx, cy),
-            floats(3, cx * 7 // 32, cy),
-            pltpu.VMEM((cx * 7 // 32, cy), jnp.int32),
+            floats(3, cx // 4, cy),
             floats(2, 8, 128),
             floats(8, 8, 128),
             floats(4, 8, 128),
             floats(3, cx // 2, cy),
             floats(3, cx // 8, cy),
             floats(cx // 2, cy),
-            floats(2 * cx, cy),
+            floats(cx // 2, cy),
             sems((4,)),
             sems((4, 3, 4)),
             sems((4, 2, 4)),
             sems((4,)),
             sems((4,)),
+            sems((3,)),
+            sems((3,)),
             sems((7,)),
             sems((7,)),
             sems((3,)),
@@ -553,12 +624,12 @@
             sems((2, 3)),
             sems((2, 3)),
             sems((2, 3)),
-            sems((3,)),
+            sems((2,)),
         ],
         compiler_params=pltpu.CompilerParams(
-            collective_id=0, has_side_effects=True, vmem_limit_bytes=60 << 20
+            collective_id=0, has_side_effects=True, vmem_limit_bytes=24 << 20
         ),
-    )(reluctivity, rotor_shift, labels, magnet_mask, potential, adjoint_load)
+    )(reluctivity, rotor_shift, *[pltpu.with_memory_space_constraint(v, pltpu.HBM) for v in (labels, magnet_mask, potential, adjoint_load)])
 
 
 def solution(mesh):

time: 76.9 us -> 74.2 us (0.965)
  Pallas kernels: 72.8 us -> 71.2 us
  local copies, waits for them, and re-layouts: 2.72 us -> 1.59 us
    pallas_call x1, Pallas kernels: 72.8 us -> 71.2 us  [local(): pl.pallas_call(kernel, out_shape=(jax.ShapeDtypeStruct(labels.shape, jnp....]
    unnamed x4, local copies, waits for them, and re-layouts: 2.72 us -> 1.59 us
where the time goes in v4:
time: 74.2 us; the launch traced here: 74.1 us
  Pallas kernels  71.2 us (96%)
  local copies, waits for them, and re-layouts  1.59 us (2%)
  between operations  1.31 us (2%)
    pallas_call x1, Pallas kernels, local(): pl.pallas_call(kernel, out_shape=(jax.ShapeDtypeStruct(labels.shape, jnp....  71.2 us
    unnamed x4, local copies, waits for them, and re-layouts  1.59 us

profile of v4, /device:TPU:4, one launch (start us, length us, event | category | flops | bytes accessed | tf_op | source)
XLA Modules:
  0.0 74.1 jit_solution(6741138515904640880)
XLA Ops:
  0.6 0.0 copy-start
  1.3 0.0 copy-done
  1.3 71.2 %shard_map.77 = (f32[2,256,256]{2,1,0:T(8,128)S(1)}, f32[1,2,256,256]{3,2,1,0:T(8,128)S(1)}) custom-call(f32[4]{0:T(128)S(1)} %copy-done, s32[1]{0:T(128)S(6)} %copy.10.shift, s32[2,256,256]{2,1,0:T(8,128)} %labels.1, s32[2,256,256]{2,1,0:T(8,128)} %mask.1, f32[1,2,256,256]{3,2,1,0:T(8,128)} %potential.1, f32[1,2,256,256]{3,2,1,0:T(8,128)} %load.1), custom_call_target="tpu_custom_call" | custom-call | tf_op jit(solution)/shard_map/pallas_call | solution.py:587
  72.5 0.8 %copy.11 = f32[2,256,256]{2,1,0:T(8,128)} copy(f32[2,256,256]{2,1,0:T(8,128)S(1)} %get-tuple-element.4) | data formatting | bytes 1048576
  73.3 0.8 %copy.12 = f32[1,2,256,256]{3,2,1,0:T(8,128)} copy(f32[1,2,256,256]{3,2,1,0:T(8,128)S(1)} %get-tuple-element.5) | data formatting | bytes 1048576
Async XLA Ops:
  0.6 0.7 copy-start

commit v5 on v4

--- a/solution.py
+++ b/solution.py
@@ -506,76 +506,89 @@
 
     quarter, small = 2 * cx // 4, 2 * cx // 16
 
-    def scatter(mine, index, peer, source, size, box, send, recv):
-        return [
-            pltpu.make_async_remote_copy(
-                src_ref=source.at[pl.ds(pl.multiple_of(index(o) * size, size), size)],
-                dst_ref=box.at[o - 1],
-                send_sem=send.at[0, o - 1],
-                recv_sem=recv.at[0, o - 1],
-                device_id=peer(o),
-                device_id_type=MESH,
+    def x_peer(o):
+        return {"pos": z_lo * 4 + x_index(o)}
+
+    def z_peer(o):
+        return {"pos": z_index(o) * 4 + x}
+
+    def remote(source, target, send, recv, peer):
+        return pltpu.make_async_remote_copy(
+            src_ref=source, dst_ref=target, send_sem=send, recv_sem=recv, device_id=peer, device_id_type=MESH
+        )
+
+    def rows_of(index):
+        return pl.ds(pl.multiple_of(index * small, small), small)
+
+    order = (1, 2, 3, 0)
+    along_x = {
+        oz: [
+            remote(
+                term.at[rows_of(x_index(o) * 4 + z_index(oz))],
+                part_x.at[o - 1, rows_of(z_index(oz))],
+                x_send.at[0, oz, o - 1],
+                x_recv.at[0, oz, o - 1],
+                x_peer(o),
             )
             for o in range(1, 4)
         ]
-
-    def x_peer(o):
-        return {"pos": z_lo * 4 + x_index(o)}
-
-    def z_peer(o):
-        return {"pos": z_index(o) * 4 + x}
-
-    copies = scatter(x, x_index, x_peer, term, quarter, part_x, x_send, x_recv)
-    for copy in copies:
+        for oz in order
+    }
+    for oz in order:
+        for copy in along_x[oz]:
+            copy.start()
+    along_z = []
+    for oz in order:
+        for copy in along_x[oz]:
+            copy.wait_recv()
+        where = rows_of(z_index(oz))
+        total = term[rows_of(x * 4 + z_index(oz)), :]
+        for o in range(3):
+            total += part_x[o, where, :]
+        piece[where, :] = total
+        if oz:
+            copy = remote(
+                piece.at[where], part_z.at[oz - 1], z_send.at[0, oz - 1], z_recv.at[0, oz - 1], z_peer(oz)
+            )
+            copy.start()
+            along_z.append(copy)
+    for oz in order:
+        for copy in along_x[oz]:
+            copy.wait_send()
+    for o, copy in enumerate(along_z):
+        copy.wait()
+        total += part_z[o]
+    mine = rows_of(z_lo)
+    merged[mine, :] = total / lax.axis_size("pos")
+
+    def place(index):
+        row = lax.rem(x, 2) * quarter + index * small
+        return gradient.at[x // 2, pl.ds(pl.multiple_of(row, small), small)]
+
+    gather_z = [
+        remote(merged.at[mine], merged.at[mine], z_send.at[1, o - 1], z_recv.at[1, o - 1], z_peer(o))
+        for o in range(1, 4)
+    ]
+    for copy in gather_z:
         copy.start()
-    for copy in copies:
+    gather_x, keeps = [], []
+    for oz in range(4):
+        index = lax.rem(z_lo + 4 - oz, 4)
+        if oz:
+            gather_z[oz - 1].wait_recv()
+        for o in range(1, 4):
+            copy = remote(
+                merged.at[rows_of(index)], place(index), x_send.at[1, oz, o - 1], x_recv.at[1, oz, o - 1], x_peer(o)
+            )
+            copy.start()
+            gather_x.append(copy)
+        keep = pltpu.make_async_copy(merged.at[rows_of(index)], place(index), out_sem.at[1 + oz])
+        keep.start()
+        keeps.append(keep)
+    for copy in gather_x + keeps:
         copy.wait()
-
-    @pl.loop(0, quarter // ROWS)
-    def _(i):
-        r = pl.multiple_of(i * ROWS, ROWS)
-        own = term[pl.ds(pl.multiple_of(x * quarter + r, ROWS), ROWS), :]
-        for o in range(3):
-            own += part_x[o, pl.ds(r, ROWS), :]
-        piece[pl.ds(r, ROWS), :] = own
-
-    copies = scatter(z_lo, z_index, z_peer, piece, small, part_z, z_send, z_recv)
-    for copy in copies:
-        copy.start()
-    for copy in copies:
-        copy.wait()
-
-    own_small = pl.ds(pl.multiple_of(z_lo * small, small), small)
-    total = piece[own_small, :]
-    for o in range(3):
-        total += part_z[o]
-    merged[own_small, :] = total / lax.axis_size("pos")
-    own_quarter = gradient.at[x // 2, pl.ds(pl.multiple_of(lax.rem(x, 2) * quarter, quarter), quarter)]
-
-    def spread(source, target, peer, send, recv):
-        copies = [
-            pltpu.make_async_remote_copy(
-                src_ref=source,
-                dst_ref=target,
-                send_sem=send.at[1, o - 1],
-                recv_sem=recv.at[1, o - 1],
-                device_id=peer(o),
-                device_id_type=MESH,
-            )
-            for o in range(1, 4)
-        ]
-        for copy in copies:
-            copy.start()
-        return copies
-
-    for copy in spread(merged.at[own_small], merged.at[own_small], z_peer, z_send, z_recv):
-        copy.wait()
-    copies = spread(merged, own_quarter, x_peer, x_send, x_recv)
-    keep = pltpu.make_async_copy(merged, own_quarter, out_sem.at[1])
-    keep.start()
-    for copy in copies:
-        copy.wait()
-    keep.wait()
+    for copy in gather_z:
+        copy.wait_send()
     finish.wait()
 
 
@@ -620,11 +633,11 @@
             sems((7,)),
             sems((3,)),
             sems((3,)),
+            sems((2, 4, 3)),
+            sems((2, 4, 3)),
             sems((2, 3)),
             sems((2, 3)),
-            sems((2, 3)),
-            sems((2, 3)),
-            sems((2,)),
+            sems((5,)),
         ],
         compiler_params=pltpu.CompilerParams(
             collective_id=0, has_side_effects=True, vmem_limit_bytes=24 << 20

time: 74.2 us -> 71.5 us (0.964)
  Pallas kernels: 71.2 us -> 68.4 us
    pallas_call x1, Pallas kernels: 71.2 us -> 68.4 us  [local(): pl.pallas_call(kernel, out_shape=(jax.ShapeDtypeStruct(labels.shape, jnp....]
where the time goes in v5:
time: 71.5 us; the launch traced here: 71.4 us
  Pallas kernels  68.4 us (96%)
  local copies, waits for them, and re-layouts  1.59 us (2%)
  between operations  1.31 us (2%)
    pallas_call x1, Pallas kernels, local(): pl.pallas_call(kernel, out_shape=(jax.ShapeDtypeStruct(labels.shape, jnp....  68.4 us
    unnamed x4, local copies, waits for them, and re-layouts  1.59 us

profile of v5, /device:TPU:4, one launch (start us, length us, event | category | flops | bytes accessed | tf_op | source)
XLA Modules:
  0.0 71.4 jit_solution(678316268204844888)
XLA Ops:
  0.6 0.0 copy-start
  1.3 0.0 copy-done
  1.3 68.4 %shard_map.77 = (f32[2,256,256]{2,1,0:T(8,128)S(1)}, f32[1,2,256,256]{3,2,1,0:T(8,128)S(1)}) custom-call(f32[4]{0:T(128)S(1)} %copy-done, s32[1]{0:T(128)S(6)} %copy.10.shift, s32[2,256,256]{2,1,0:T(8,128)} %labels.1, s32[2,256,256]{2,1,0:T(8,128)} %mask.1, f32[1,2,256,256]{3,2,1,0:T(8,128)} %potential.1, f32[1,2,256,256]{3,2,1,0:T(8,128)} %load.1), custom_call_target="tpu_custom_call" | custom-call | tf_op jit(solution)/shard_map/pallas_call | solution.py:600
  69.8 0.8 %copy.11 = f32[2,256,256]{2,1,0:T(8,128)} copy(f32[2,256,256]{2,1,0:T(8,128)S(1)} %get-tuple-element.4) | data formatting | bytes 1048576
  70.6 0.8 %copy.12 = f32[1,2,256,256]{3,2,1,0:T(8,128)} copy(f32[1,2,256,256]{3,2,1,0:T(8,128)S(1)} %get-tuple-element.5) | data formatting | bytes 1048576
Async XLA Ops:
  0.6 0.7 copy-start

commit v6 on v5

--- a/solution.py
+++ b/solution.py
@@ -7,7 +7,7 @@
 
 MESH = pl.DeviceIdType.MESH
 PAD = 8
-ROWS = 32
+ROWS = 128
 diagonal_shift = 0.5
 
 
@@ -19,7 +19,7 @@
 
 def kernel(
     reluctivity, shift, labels, mask, potential, load, gradient, adjoint,
-    label_x, nu_x, d_x, w_x, a_x, pot_x, mask_x, term, relay, tile, near, far,
+    label_x, nu_x, d_x, w_x, a_x, pot_x, mask_x, term, fields, relay, tile, near, far,
     part_x, part_z, piece, merged, local_sem, send_sem, recv_sem, relay_send, relay_recv, share_send, share_recv,
     near_send, near_recv, far_send, far_recv, x_send, x_recv, z_send, z_recv, out_sem,
 ):
@@ -299,7 +299,7 @@
     label_halo.start()
     d_halo.start()
 
-    for ref in (nu_x, d_x, w_x, a_x, pot_x):
+    for ref in (nu_x, d_x, w_x, pot_x):
         for layer in (1, 2):
             ref[layer, pl.ds(0, PAD), :] = jnp.zeros((PAD, cy), jnp.float32)
             ref[layer, pl.ds(PAD + cx, PAD), :] = jnp.zeros((PAD, cy), jnp.float32)
@@ -366,14 +366,15 @@
             w_x[layer, pl.ds(PAD + r, ROWS), :] = image
 
     w_halo.start()
+    pot_halo.start()
     label_halo.relay()
     d_halo.relay()
     w_halo.relay()
+    pot_halo.relay()
     label_halo.wait()
     materials((0, 3))
     d_halo.wait()
     w_halo.wait()
-    pot_halo.start()
 
     def sides(ref, layer, r):
         below, above = at(ref, layer - 1, r), at(ref, layer + 1, r)
@@ -456,35 +457,23 @@
         for copy in copies:
             copy.start()
         box[mine] = tile[stage]
-        for copy in copies:
-            copy.wait()
-        return combine(box)
+
+        def finish():
+            for copy in copies:
+                copy.wait()
+            return combine(box)
+
+        return finish
 
     values = (theta, norm, *[whole_sum(part) for part in sums])
-    values = exchange(0, values, 8, inner, near, near_peer, near_send, near_recv)
-    pot_halo.relay()
-    values = exchange(1, values, 4, z_hi, far, far_peer, far_send, far_recv)
-    centre, m0, _, m2, m3, _ = values
-    alpha0 = 1.0 / centre
-    beta = alpha0 * alpha0 * m2 / m0
-    alpha1 = m2 / (m3 - alpha0 * m2 * (m2 / m0))
-    from_d = wide(alpha0 + alpha1 * (1.0 + beta))
-    from_w = wide(alpha0 * alpha1)
-
-    @pl.loop(0, cx // ROWS)
-    def _(i):
-        r = pl.multiple_of(i * ROWS, ROWS)
-        for layer in range(4):
-            value = from_d * at(d_x, layer, r) - from_w * at(w_x, layer, r)
-            a_x[layer, pl.ds(PAD + r, ROWS), :] = value * live[layer]
-
-    finish = pltpu.make_async_copy(a_x.at[pl.ds(1, 2), pl.ds(PAD, cx)], adjoint.at[0], out_sem.at[0])
-    finish.start()
+    values = exchange(0, values, 8, inner, near, near_peer, near_send, near_recv)()
+    arrive = exchange(1, values, 4, z_hi, far, far_peer, far_send, far_recv)
     local[2].wait()
     local[3].wait()
     pot_halo.wait()
 
-    def slopes(ref, layer, r, below, above):
+    def slopes(ref, layer, r):
+        below, above = sides(ref, layer, r)
         v_tall = tall(ref, layer, r)
         v = middle(v_tall)
         return (
@@ -497,12 +486,27 @@
     def _(i):
         r = pl.multiple_of(i * ROWS, ROWS)
         for layer in (1, 2):
-            pot = slopes(pot_x, layer, r, *sides(pot_x, layer, r))
-            adj = slopes(a_x, layer, r, at(a_x, layer - 1, r), at(a_x, layer + 1, r))
-            total = sum(p * (a + 0.5 * p) for p, a in zip(pot, adj))
             chosen = mask_x[layer - 1, pl.ds(r, ROWS), :].astype(jnp.float32)
-            value = 0.25 * chosen * at(nu_x, layer, r) * total
-            term[pl.ds((layer - 1) * cx + r, ROWS), :] = value
+            weight = 0.25 * chosen * at(nu_x, layer, r)
+            pot = slopes(pot_x, layer, r)
+            where = pl.ds((layer - 1) * cx + r, ROWS)
+            for index, ref in enumerate((d_x, w_x)):
+                other = slopes(ref, layer, r)
+                fields[index, where, :] = weight * sum(p * q for p, q in zip(pot, other))
+            fields[2, where, :] = 0.5 * weight * sum(p * p for p in pot)
+
+    values = arrive()
+    centre, m0, _, m2, m3, _ = values
+    alpha0 = 1.0 / centre
+    beta = alpha0 * alpha0 * m2 / m0
+    alpha1 = m2 / (m3 - alpha0 * m2 * (m2 / m0))
+    from_d = wide(alpha0 + alpha1 * (1.0 + beta))
+    from_w = wide(alpha0 * alpha1)
+
+    @pl.loop(0, 2 * cx // ROWS)
+    def _(i):
+        rows = pl.ds(pl.multiple_of(i * ROWS, ROWS), ROWS)
+        term[rows, :] = from_d * fields[0, rows, :] - from_w * fields[1, rows, :] + fields[2, rows, :]
 
     quarter, small = 2 * cx // 4, 2 * cx // 16
 
@@ -537,6 +541,16 @@
     for oz in order:
         for copy in along_x[oz]:
             copy.start()
+
+    @pl.loop(0, cx // ROWS)
+    def _(i):
+        r = pl.multiple_of(i * ROWS, ROWS)
+        for layer in (1, 2):
+            value = from_d * at(d_x, layer, r) - from_w * at(w_x, layer, r)
+            a_x[layer - 1, pl.ds(r, ROWS), :] = value
+
+    finish = pltpu.make_async_copy(a_x, adjoint.at[0], out_sem.at[0])
+    finish.start()
     along_z = []
     for oz in order:
         for copy in along_x[oz]:
@@ -610,10 +624,11 @@
             floats(4, tall, cy),
             floats(4, tall, cy),
             floats(4, tall, cy),
-            floats(4, tall, cy),
+            floats(2, cx, cy),
             floats(4, tall, cy),
             pltpu.VMEM((2, cx, cy), jnp.int32),
             floats(2 * cx, cy),
+            floats(3, 2 * cx, cy),
             floats(3, cx // 4, cy),
             floats(2, 8, 128),
             floats(8, 8, 128),

time: 71.5 us -> 67.8 us (0.948)
  Pallas kernels: 68.4 us -> 64.7 us
    pallas_call x1, Pallas kernels: 68.4 us -> 64.7 us  [local(): pl.pallas_call(kernel, out_shape=(jax.ShapeDtypeStruct(labels.shape, jnp....]
where the time goes in v6:
time: 67.8 us; the launch traced here: 67.6 us
  Pallas kernels  64.7 us (95%)
  local copies, waits for them, and re-layouts  1.59 us (2%)
  between operations  1.31 us (2%)
    pallas_call x1, Pallas kernels, local(): pl.pallas_call(kernel, out_shape=(jax.ShapeDtypeStruct(labels.shape, jnp....  64.7 us
    unnamed x4, local copies, waits for them, and re-layouts  1.59 us

profile of v6, /device:TPU:4, one launch (start us, length us, event | category | flops | bytes accessed | tf_op | source)
XLA Modules:
  0.0 67.6 jit_solution(14835859836358261455)
XLA Ops:
  0.6 0.0 copy-start
  1.3 0.0 copy-done
  1.3 64.7 %shard_map.77 = (f32[2,256,256]{2,1,0:T(8,128)S(1)}, f32[1,2,256,256]{3,2,1,0:T(8,128)S(1)}) custom-call(f32[4]{0:T(128)S(1)} %copy-done, s32[1]{0:T(128)S(6)} %copy.10.shift, s32[2,256,256]{2,1,0:T(8,128)} %labels.1, s32[2,256,256]{2,1,0:T(8,128)} %mask.1, f32[1,2,256,256]{3,2,1,0:T(8,128)} %potential.1, f32[1,2,256,256]{3,2,1,0:T(8,128)} %load.1), custom_call_target="tpu_custom_call" | custom-call | tf_op jit(solution)/shard_map/pallas_call | solution.py:614
  66.0 0.8 %copy.11 = f32[2,256,256]{2,1,0:T(8,128)} copy(f32[2,256,256]{2,1,0:T(8,128)S(1)} %get-tuple-element.4) | data formatting | bytes 1048576
  66.8 0.8 %copy.12 = f32[1,2,256,256]{3,2,1,0:T(8,128)} copy(f32[1,2,256,256]{3,2,1,0:T(8,128)S(1)} %get-tuple-element.5) | data formatting | bytes 1048576
Async XLA Ops:
  0.6 0.7 copy-start

commit v7 on v6

--- a/solution.py
+++ b/solution.py
@@ -19,9 +19,9 @@
 
 def kernel(
     reluctivity, shift, labels, mask, potential, load, gradient, adjoint,
-    label_x, nu_x, d_x, w_x, a_x, pot_x, mask_x, term, fields, relay, tile, near, far,
+    label_x, nu_x, d_x, w_x, a_x, pot_x, mask_x, term, fields, relay, tile, box,
     part_x, part_z, piece, merged, local_sem, send_sem, recv_sem, relay_send, relay_recv, share_send, share_recv,
-    near_send, near_recv, far_send, far_recv, x_send, x_recv, z_send, z_recv, out_sem,
+    all_send, all_recv, x_send, x_recv, z_send, z_recv, out_sem,
 ):
     pos, slab = lax.axis_index("pos"), lax.axis_index("slab")
     n_slab = lax.axis_size("slab")
@@ -44,11 +44,8 @@
     for copy in local:
         copy.start()
 
-    def near_peer(o):
-        return {"slab": z_hi * 8 + lax.rem(inner + o, 8)}
-
-    def far_peer(o):
-        return {"slab": lax.rem(z_hi + o, 4) * 8 + inner}
+    offsets = [8 * o + i for o in (2, 1, 3) for i in range(8)] + list(range(1, 8))
+    members = [{"slab": lax.rem(z_hi + c // 8, 4) * 8 + lax.rem(inner + c % 8, 8)} for c in offsets]
 
     def x_index(o):
         return lax.rem(x + o, 4)
@@ -56,9 +53,7 @@
     def z_index(o):
         return lax.rem(z_lo + o, 4)
 
-    peers = [{"slab": up}, {"slab": down}]
-    peers += [near_peer(o) for o in range(1, 8)]
-    peers += [far_peer(o) for o in range(1, 4)]
+    peers = list(members)
     peers += [{"pos": z_lo * 4 + x_index(o)} for o in range(1, 4)]
     peers += [{"pos": z_index(o) * 4 + x} for o in range(1, 4)]
     barrier = pltpu.get_barrier_semaphore()
@@ -74,26 +69,7 @@
     for peer in peers:
         greet(peer)
 
-    @pl.when(is_first)
-    def _():
-        for i in (1, 3, 5):
-            greet({"slab": z_down + i})
-
-    @pl.when(is_last)
-    def _():
-        for i in (2, 4, 6):
-            greet({"slab": z_up + i})
-
-    @pl.when(is_up_relay)
-    def _():
-        greet({"slab": z_up})
-
-    @pl.when(is_down_relay)
-    def _():
-        greet({"slab": z_down + 7})
-
-    ends = jnp.logical_or(is_first, is_last)
-    pl.semaphore_wait(barrier, len(peers) + jnp.where(ends, 3, 1))
+    pl.semaphore_wait(barrier, len(peers))
     strip = cx // 4
     row = inner // 2
 
@@ -425,8 +401,10 @@
 
     sums = lax.fori_loop(0, cx // ROWS, second_pass, (zero,) * 4)
 
-    def combine(box):
-        th, m0, m1, m2, m3, m4 = [box[:, i, :] for i in range(6)]
+    def combine():
+        rows = box[:, 0, :]
+        width = rows.shape[1]
+        th, m0, m1, m2, m3, m4 = [pltpu.roll(rows, (width - i) % width, 1) for i in range(6)]
         total = lambda value: jnp.sum(value, axis=0, keepdims=True)
         centre = quotient(total(th * m0 + m1), total(m0))
         e = centre - th
@@ -434,40 +412,42 @@
         return (
             centre,
             total(m0),
-            total(m1 - e * m0),
             total(m2 - e * (2.0 * m1 - e * m0)),
             total(m3 - e * (m2 + th * m1 + m4 - e * dw)),
-            total(m4 - e * dw),
         )
 
-    def exchange(stage, values, size, mine, box, peer, send, recv):
-        for i, value in enumerate(values):
-            tile[stage, pl.ds(i, 1), :] = wide(value, tile.shape[2])
+    def exchange(values):
+        lane = lax.broadcasted_iota(jnp.int32, (1, tile.shape[1]), 1)
+        packed = wide(values[0], tile.shape[1])
+        for i, value in enumerate(values[1:], 1):
+            packed = jnp.where(lane == i, wide(value, tile.shape[1]), packed)
+        line = pl.ds(0, 1)
+        tile[line, :] = packed
         copies = [
             pltpu.make_async_remote_copy(
-                src_ref=tile.at[stage],
-                dst_ref=box.at[mine],
-                send_sem=send.at[o - 1],
-                recv_sem=recv.at[o - 1],
-                device_id=peer(o),
+                src_ref=tile.at[line],
+                dst_ref=box.at[slab, line],
+                send_sem=all_send.at[k],
+                recv_sem=all_recv.at[k],
+                device_id=peer,
                 device_id_type=MESH,
             )
-            for o in range(1, size)
+            for k, peer in enumerate(members)
         ]
         for copy in copies:
             copy.start()
-        box[mine] = tile[stage]
+        box[slab, line, :] = packed
 
         def finish():
             for copy in copies:
-                copy.wait()
-            return combine(box)
+                copy.wait_recv()
+            result = combine()
+            return result, copies
 
         return finish
 
     values = (theta, norm, *[whole_sum(part) for part in sums])
-    values = exchange(0, values, 8, inner, near, near_peer, near_send, near_recv)()
-    arrive = exchange(1, values, 4, z_hi, far, far_peer, far_send, far_recv)
+    arrive = exchange(values)
     local[2].wait()
     local[3].wait()
     pot_halo.wait()
@@ -495,8 +475,8 @@
                 fields[index, where, :] = weight * sum(p * q for p, q in zip(pot, other))
             fields[2, where, :] = 0.5 * weight * sum(p * p for p in pot)
 
-    values = arrive()
-    centre, m0, _, m2, m3, _ = values
+    values, sent = arrive()
+    centre, m0, m2, m3 = values
     alpha0 = 1.0 / centre
     beta = alpha0 * alpha0 * m2 / m0
     alpha1 = m2 / (m3 - alpha0 * m2 * (m2 / m0))
@@ -551,6 +531,8 @@
 
     finish = pltpu.make_async_copy(a_x, adjoint.at[0], out_sem.at[0])
     finish.start()
+    for copy in sent:
+        copy.wait_send()
     along_z = []
     for oz in order:
         for copy in along_x[oz]:
@@ -630,9 +612,8 @@
             floats(2 * cx, cy),
             floats(3, 2 * cx, cy),
             floats(3, cx // 4, cy),
-            floats(2, 8, 128),
-            floats(8, 8, 128),
-            floats(4, 8, 128),
+            floats(8, 128),
+            floats(32, 8, 128),
             floats(3, cx // 2, cy),
             floats(3, cx // 8, cy),
             floats(cx // 2, cy),
@@ -644,10 +625,8 @@
             sems((4,)),
             sems((3,)),
             sems((3,)),
-            sems((7,)),
-            sems((7,)),
-            sems((3,)),
-            sems((3,)),
+            sems((31,)),
+            sems((31,)),
             sems((2, 4, 3)),
             sems((2, 4, 3)),
             sems((2, 3)),

time: 67.8 us -> 67 us (0.988)
  Pallas kernels: 64.7 us -> 63.9 us
    pallas_call x1, Pallas kernels: 64.7 us -> 63.9 us  [local(): pl.pallas_call(kernel, out_shape=(jax.ShapeDtypeStruct(labels.shape, jnp....]
where the time goes in v7:
time: 67 us; the launch traced here: 66.8 us
  Pallas kernels  63.9 us (95%)
  local copies, waits for them, and re-layouts  1.59 us (2%)
  between operations  1.31 us (2%)
    pallas_call x1, Pallas kernels, local(): pl.pallas_call(kernel, out_shape=(jax.ShapeDtypeStruct(labels.shape, jnp....  63.9 us
    unnamed x4, local copies, waits for them, and re-layouts  1.59 us

profile of v7, /device:TPU:4, one launch (start us, length us, event | category | flops | bytes accessed | tf_op | source)
XLA Modules:
  0.0 66.8 jit_solution(11439907946196668364)
XLA Ops:
  0.6 0.0 copy-start
  1.3 0.0 copy-done
  1.3 63.9 %shard_map.77 = (f32[2,256,256]{2,1,0:T(8,128)S(1)}, f32[1,2,256,256]{3,2,1,0:T(8,128)S(1)}) custom-call(f32[4]{0:T(128)S(1)} %copy-done, s32[1]{0:T(128)S(6)} %copy.10.shift, s32[2,256,256]{2,1,0:T(8,128)} %labels.1, s32[2,256,256]{2,1,0:T(8,128)} %mask.1, f32[1,2,256,256]{3,2,1,0:T(8,128)} %potential.1, f32[1,2,256,256]{3,2,1,0:T(8,128)} %load.1), custom_call_target="tpu_custom_call" | custom-call | tf_op jit(solution)/shard_map/pallas_call | solution.py:596
  65.2 0.8 %copy.11 = f32[2,256,256]{2,1,0:T(8,128)} copy(f32[2,256,256]{2,1,0:T(8,128)S(1)} %get-tuple-element.4) | data formatting | bytes 1048576
  66.0 0.8 %copy.12 = f32[1,2,256,256]{3,2,1,0:T(8,128)} copy(f32[1,2,256,256]{3,2,1,0:T(8,128)S(1)} %get-tuple-element.5) | data formatting | bytes 1048576
Async XLA Ops:
  0.6 0.7 %copy-start = (f32[4]{0:T(128)S(1)}, f32[4]{0:T(128)}, u32[]{:S(2)}) copy-start(f32[4]{0:T(128)} %reluctivity.1) | copy-start | bytes 52

commit v8 on v7

--- a/solution.py
+++ b/solution.py
@@ -483,10 +483,8 @@
     from_d = wide(alpha0 + alpha1 * (1.0 + beta))
     from_w = wide(alpha0 * alpha1)
 
-    @pl.loop(0, 2 * cx // ROWS)
-    def _(i):
-        rows = pl.ds(pl.multiple_of(i * ROWS, ROWS), ROWS)
-        term[rows, :] = from_d * fields[0, rows, :] - from_w * fields[1, rows, :] + fields[2, rows, :]
+    def blend(rows):
+        return from_d * fields[0, rows, :] - from_w * fields[1, rows, :] + fields[2, rows, :]
 
     quarter, small = 2 * cx // 4, 2 * cx // 16
 
@@ -519,7 +517,9 @@
         for oz in order
     }
     for oz in order:
-        for copy in along_x[oz]:
+        for o, copy in enumerate(along_x[oz], 1):
+            rows = rows_of(x_index(o) * 4 + z_index(oz))
+            term[rows, :] = blend(rows)
             copy.start()
 
     @pl.loop(0, cx // ROWS)
@@ -538,7 +538,7 @@
         for copy in along_x[oz]:
             copy.wait_recv()
         where = rows_of(z_index(oz))
-        total = term[rows_of(x * 4 + z_index(oz)), :]
+        total = blend(rows_of(x * 4 + z_index(oz)))
         for o in range(3):
             total += part_x[o, where, :]
         piece[where, :] = total

time: 67 us -> 66.7 us (level)
  no operation moved by 1% of the time
where the time goes in v8:
time: 66.7 us; the launch traced here: 66.5 us
  Pallas kernels  63.6 us (95%)
  local copies, waits for them, and re-layouts  1.59 us (2%)
  between operations  1.31 us (2%)
    pallas_call x1, Pallas kernels, local(): pl.pallas_call(kernel, out_shape=(jax.ShapeDtypeStruct(labels.shape, jnp....  63.6 us
    unnamed x4, local copies, waits for them, and re-layouts  1.59 us

profile of v8, /device:TPU:4, one launch (start us, length us, event | category | flops | bytes accessed | tf_op | source)
XLA Modules:
  0.0 66.5 jit_solution(2133321595512016347)
XLA Ops:
  0.6 0.0 copy-start
  1.3 0.0 copy-done
  1.3 63.6 %shard_map.77 = (f32[2,256,256]{2,1,0:T(8,128)S(1)}, f32[1,2,256,256]{3,2,1,0:T(8,128)S(1)}) custom-call(f32[4]{0:T(128)S(1)} %copy-done, s32[1]{0:T(128)S(6)} %copy.10.shift, s32[2,256,256]{2,1,0:T(8,128)} %labels.1, s32[2,256,256]{2,1,0:T(8,128)} %mask.1, f32[1,2,256,256]{3,2,1,0:T(8,128)} %potential.1, f32[1,2,256,256]{3,2,1,0:T(8,128)} %load.1), custom_call_target="tpu_custom_call" | custom-call | tf_op jit(solution)/shard_map/pallas_call | solution.py:596
  64.9 0.8 %copy.11 = f32[2,256,256]{2,1,0:T(8,128)} copy(f32[2,256,256]{2,1,0:T(8,128)S(1)} %get-tuple-element.4) | data formatting | bytes 1048576
  65.7 0.8 %copy.12 = f32[1,2,256,256]{3,2,1,0:T(8,128)} copy(f32[1,2,256,256]{3,2,1,0:T(8,128)S(1)} %get-tuple-element.5) | data formatting | bytes 1048576
Async XLA Ops:
  0.6 0.7 %copy-start = (f32[4]{0:T(128)S(1)}, f32[4]{0:T(128)}, u32[]{:S(2)}) copy-start(f32[4]{0:T(128)} %reluctivity.1) | copy-start | bytes 52
